TPU v7x, 512 devices: a whole 4x4x16 slice. The times are simulated.
512 devices in a mesh: lag: 64 (over z, y), par: 8 (over x, core).
Axes of the slice: x: 4, y: 4, z: 16, core: 2. Of those that a mesh axis runs over, the one named last changes fastest.
Arguments:
- prior_rows: bfloat16 [64, 512, 16384], P('lag', None, 'par'), may hold values from -0.0625 to 0.0625
- raw_rows: bfloat16 [64, 512, 16384], P('lag', None, 'par'), may hold values from -6 to 6
Outputs:
- diag_zero: float32 [64, 512, 512], P('lag', 'par')
- diag_one: float32 [64, 512, 512], P('lag', 'par')
All inputs are finite; a program needn't handle non-finite values.
Results may differ from a plain program's by a relative error of at most 0.0003.
Values may be sent and summed in bfloat16 or wider, within the bound.
No kernel may reach another device: no remote copies, remote signals or barrier semaphores. Data moves between devices by JAX's collectives and lax.ppermute only.
A program may use at most 64 MiB of HBM per device.

v0:
```python
import jax
import jax.numpy as jnp
from jax import lax
from jax.sharding import PartitionSpec as P


def passed_along(block, axis, distance):
    devices = range(lax.axis_size(axis))
    route = [(i - distance, i) for i in devices if i - distance in devices]
    return lax.ppermute(block, axis, route)


def carried_in(part, axis, combine, identity):
    place = lax.axis_index(axis)
    gathered = lax.all_gather(part, axis)
    state = jnp.zeros_like(part) + jnp.asarray(identity, part.dtype)

    def one(turn, state):
        return combine(state, lax.dynamic_index_in_dim(gathered, turn, 0, False))

    return lax.fori_loop(0, place, one, state)


def add_terms(earlier_term, later_term):
    return earlier_term + later_term


def body(prior_rows, raw_rows):
    incoming = passed_along(raw_rows, "lag", -1)
    following = jnp.concatenate([raw_rows[1:], incoming], axis=0)
    offset_zero = jnp.einsum(
        "lsp,ltp->lst", prior_rows, raw_rows, preferred_element_type=jnp.float32
    )
    offset_one = jnp.einsum(
        "lsp,ltp->lst", prior_rows, following, preferred_element_type=jnp.float32
    )
    stacked = jnp.stack([offset_zero, offset_one], axis=0)
    summed = lax.psum(stacked, "par")
    row_count = summed.shape[2] // lax.axis_size("par")
    shares = lax.dynamic_slice_in_dim(summed, lax.axis_index("par") * row_count, row_count, 2)
    running = jnp.cumsum(shares, axis=1)
    totals = running[:, -1]
    earlier = carried_in(totals, "lag", add_terms, jnp.zeros_like(totals))
    result = running + earlier[:, None]
    return (result[0], result[1])


def solution(mesh):
    in_specs = (P("lag", None, "par"), P("lag", None, "par"))
    out_specs = (P("lag", "par", None), P("lag", "par", None))
    return jax.shard_map(body, mesh=mesh, in_specs=in_specs, out_specs=out_specs, check_vma=False)
```

profile of v0, /device:TPU:504, one launch (start us, length us, event | category | flops | bytes accessed | tf_op | source)
XLA Modules:
  0.0 406.9 jit_solution(13441115809973751010)
XLA Ops:
  7.2 2.9 collective-permute-start
  10.2 2.9 fusion.6
  13.0 42.2 %collective-permute-done = bf16[1,512,2048]{2,1,0:T(8,128)(2,1)S(1)} collective-permute-done((bf16[1,512,2048]{2,1,0:T(8,128)(2,1)}, bf16[1,512,2048]{2,1,0:T(8,128)(2,1)S(1)}, u32[]{:S(2)}, u32[]{:S(2)}) %collective-permute-start) | collective-permute-done | bytes 2097184 | tf_op jit(solution)/shard_map/ppermute | solution.py:10
  55.2 1.3 fusion.11
  56.5 1.5 pad_maximum_fusion
  58.1 83.5 %all-reduce.2.cloned.1.call-done = f32[2,1,512,512]{3,2,1,0:T(8,128)} async-done(((f32[2,1,512,512]{3,2,1,0:T(8,128)}), f32[2,1,512,512]{3,2,1,0:T(8,128)}) %all-reduce.2.cloned.1.call-update) | async-done | bytes 2097168 | tf_op jit(solution)/shard_map/psum | solution.py:38
  141.5 1.7 constant_dynamic-slice_fusion
  143.2 189.3 %all-gather.3.cloned.1.call-done = f32[128,1,64,512]{3,2,1,0:T(8,128)} async-done(((f32[2,1,64,512]{3,2,1,0:T(8,128)}), f32[128,1,64,512]{3,2,1,0:T(8,128)}) %all-gather.3.cloned.1.call-update) | async-done | bytes 16777232 | tf_op jit(solution)/shard_map/all_gather | solution.py:15
  332.6 65.8 %while.10 = (s32[]{:T(128)}, f32[2,64,512]{2,1,0:T(8,128)S(1)}, s32[]{:T(128)}, f32[64,2,64,512]{3,2,1,0:T(8,128)}, s32[]{:T(128)}, /*index=5*/s32[]{:T(128)}, s32[]{:T(128)}) while((s32[]{:T(128)}, f32[2,64,512]{2,1,0:T(8,128)S(1)}, s32[]{:T(128)}, f32[64,2,64,512]{3,2,1,0:T(8,128)}, s32[]{:T(128)}, /*index=5*/s32[]{:T(128)}, s32[]{:T(128)}) %tuple.30), condition=%wide.region_2.3_spmd, body=%wide.region_1.0_spmd.sunk | while | flops 65541 | bytes 786555 | solution.py:21
  332.6 1.0 bitcast_add_fusion.3
  333.6 1.0 bitcast_add_fusion.3
  334.7 1.0 bitcast_add_fusion.3
  335.7 1.0 bitcast_add_fusion.3
  336.8 1.0 bitcast_add_fusion.3
  337.8 1.0 bitcast_add_fusion.3
  338.9 1.0 bitcast_add_fusion.3
  339.9 1.0 bitcast_add_fusion.3
  340.9 1.0 bitcast_add_fusion.3
  342.0 1.0 bitcast_add_fusion.3
  343.0 1.0 bitcast_add_fusion.3
  344.1 1.0 bitcast_add_fusion.3
  345.1 1.0 bitcast_add_fusion.3
  346.2 1.0 bitcast_add_fusion.3
  347.2 1.0 bitcast_add_fusion.3
  348.3 1.0 bitcast_add_fusion.3
  349.3 1.0 bitcast_add_fusion.3
  350.3 1.0 bitcast_add_fusion.3
  351.4 1.0 bitcast_add_fusion.3
  352.4 1.0 bitcast_add_fusion.3
  353.5 1.0 bitcast_add_fusion.3
  354.5 1.0 bitcast_add_fusion.3
  355.6 1.0 bitcast_add_fusion.3
  356.6 1.0 bitcast_add_fusion.3
  357.7 1.0 bitcast_add_fusion.3
  358.7 1.0 bitcast_add_fusion.3
  359.7 1.0 bitcast_add_fusion.3
  360.8 1.0 bitcast_add_fusion.3
  361.8 1.0 bitcast_add_fusion.3
  362.9 1.0 bitcast_add_fusion.3
  363.9 1.0 bitcast_add_fusion.3
  365.0 1.0 bitcast_add_fusion.3
  366.0 1.0 bitcast_add_fusion.3
  367.1 1.0 bitcast_add_fusion.3
  368.1 1.0 bitcast_add_fusion.3
  369.1 1.0 bitcast_add_fusion.3
  370.2 1.0 bitcast_add_fusion.3
  371.2 1.0 bitcast_add_fusion.3
  372.3 1.0 bitcast_add_fusion.3
  373.3 1.0 bitcast_add_fusion.3
  374.4 1.0 bitcast_add_fusion.3
  375.4 1.0 bitcast_add_fusion.3
  376.5 1.0 bitcast_add_fusion.3
  377.5 1.0 bitcast_add_fusion.3
  378.5 1.0 bitcast_add_fusion.3
  379.6 1.0 bitcast_add_fusion.3
  380.6 1.0 bitcast_add_fusion.3
  381.7 1.0 bitcast_add_fusion.3
  382.7 1.0 bitcast_add_fusion.3
  383.8 1.0 bitcast_add_fusion.3
  384.8 1.0 bitcast_add_fusion.3
  385.8 1.0 bitcast_add_fusion.3
  386.9 1.0 bitcast_add_fusion.3
  395.2 1.0 bitcast_add_fusion.3
  397.3 1.0 bitcast_add_fusion.3
  (17 shorter events, 10.0 us)
Async XLA Ops:
  7.2 3.0 copy-start
  7.2 134.4 %all-reduce.2.cloned.1.call-start = ((), (), s32[]{:S(2)}) async-start(), calls=%async_computation | async-start | bytes 4194304 | tf_op jit(solution)/shard_map/psum | solution.py:38
  7.2 48.0 %collective-permute-start = (bf16[1,512,2048]{2,1,0:T(8,128)(2,1)}, bf16[1,512,2048]{2,1,0:T(8,128)(2,1)S(1)}, u32[]{:S(2)}, u32[]{:S(2)}) collective-permute-start(bf16[1,512,2048]{2,1,0:T(8,128)(2,1)} %param.5), channel_id=1, source_target_pairs={{8,0},{16,8},{24,16},{32,24},{40,32},{48,40},{56,48},{64,56},{72,6... | collective-permute-start | bytes 6291464 | tf_op jit(solution)/shard_map/ppermute | solution.py:10
  58.0 274.5 %all-gather.3.cloned.1.call-start = ((), (), s32[]{:S(2)}) async-start(), calls=%async_computation.1 | async-start | bytes 17039360 | tf_op jit(solution)/shard_map/all_gather | solution.py:15
Sparse Core Ops, SparseCore 0:
  58.2 83.3 all-reduce.1
  144.5 188.0 all-gather.2
where the time goes:
time: 409 us; the launch traced here: 407 us
  waiting for transfers between devices  315 us (77%)
  other arithmetic  66.9 us (16%)
  between operations  14.1 us (3%)
  matrix products  4.16 us (1%)
    all_gather x1, waiting for transfers between devices, carried_in(): gathered = lax.all_gather(part, axis)  189 us
    psum x1, waiting for transfers between devices, body(): summed = lax.psum(stacked, 'par')  83.5 us
    add x63, other arithmetic, add_terms(): return earlier_term + later_term  64.4 us
    ppermute x1, waiting for transfers between devices, passed_along(): return lax.ppermute(block, axis, route)  42.2 us
  transfers between devices with their start and end apart: 3, of which 3 were waited for; matrix products, arithmetic and copies ran while one was open for 1% of the time, Pallas kernels for 0%

commit v1 on v0

v1 whole, which is shorter than its diff:
```python
import jax
import jax.numpy as jnp
import numpy as np
from jax import lax
from jax.experimental import pallas as pl
from jax.experimental.pallas import tpu as pltpu
from jax.sharding import Mesh, PartitionSpec as P

F32 = jnp.float32
NT = (((1,), (1,)), ((), ()))
LAG = ("z", "y")
PAR = ("x", "core")
VMEM = pl.BlockSpec(memory_space=pltpu.VMEM)


def call(kernel, out_shape, *args):
    return pl.pallas_call(
        kernel,
        out_shape=out_shape,
        in_specs=[VMEM] * len(args),
        out_specs=jax.tree.map(lambda _: VMEM, out_shape),
    )(*args)


def shape(*dims):
    return jax.ShapeDtypeStruct(dims, F32)


def tile_zero_kernel(prior, raw, out):
    for x in range(4):
        part = lax.dot_general(prior[x * 128 : (x + 1) * 128], raw[...], NT, preferred_element_type=F32)
        for c in range(2):
            out[c, x] = part[c * 64 : (c + 1) * 64]


def tile_one_kernel(prior, raw_next, prior_last, raw, out):
    for x in range(4):
        rows = slice(x * 128, (x + 1) * 128)
        part = lax.dot_general(prior[rows], raw_next[...], NT, preferred_element_type=F32)
        part += lax.dot_general(prior_last[rows], raw[...], NT, preferred_element_type=F32)
        for c in range(2):
            for y in range(4):
                first = c * 64 + y * 16
                out[y, x, c] = part[first : first + 16]


def add_kernel(parts, out):
    total = parts[0]
    for i in range(1, parts.shape[0]):
        total = total + parts[i]
    out[...] = total


def spread(ref, half, value, first):
    for i in range(2):
        for j in range(4):
            tile = value[i * 8 : (i + 1) * 8, j * 128 : (j + 1) * 128]
            ref[first + i * 4 + j, half * 8 : (half + 1) * 8, :] = tile


def gathered(ref, half, first):
    rows = []
    for i in range(2):
        tiles = [ref[first + i * 4 + j, half * 8 : (half + 1) * 8, :] for j in range(4)]
        rows.append(jnp.concatenate(tiles, axis=1))
    return jnp.concatenate(rows, axis=0)


def local_prefix_kernel(zero, one, local, ahead):
    total_zero, total_one, delayed = None, None, []
    for lag in range(4):
        here, late = one[lag, 0, 0], one[lag, 0, 1]
        for x in range(1, 4):
            here, late = here + one[lag, x, 0], late + one[lag, x, 1]
        total_zero = zero[lag] if lag == 0 else total_zero + zero[lag]
        local[lag, 0] = total_zero
        if lag == 0:
            spread(ahead, 1, late, 8)
            total_one = here + late
        else:
            local[lag - 1, 1] = total_one + late
            total_one = total_one + here + late
    local[3, 1] = total_one
    spread(ahead, 0, total_zero, 0)
    spread(ahead, 0, total_one, 8)
    spread(ahead, 1, jnp.zeros_like(total_zero), 0)


def lag_scan_kernel(ahead, back):
    state = jnp.zeros((8, 128), F32)
    for z in range(16):
        back[z, 0:8] = state
        state = state + ahead[z, 0:8]
        back[z, 8:16] = ahead[z + 1, 8:16] if z < 15 else jnp.zeros((8, 128), F32)


def finish_kernel(local, back, out):
    earlier_zero, earlier_one, late = gathered(back, 0, 0), gathered(back, 0, 8), gathered(back, 1, 8)
    for lag in range(4):
        out[lag, 0:16] = local[lag, 0] + earlier_zero
        last = local[lag, 1] + earlier_one
        out[lag, 16:32] = last + late if lag == 3 else last


def split_kernel(rows, zero, one):
    for y in range(4):
        zero[0, y * 16 : (y + 1) * 16] = rows[y, 0:16]
        one[0, y * 16 : (y + 1) * 16] = rows[y, 16:32]


def exchange(value, axes):
    return lax.all_to_all(value, axes, 0, 0, tiled=True)


def body(prior_rows, raw_rows):
    prior, raw = prior_rows[0], raw_rows[0]
    device = np.arange(512).reshape(64, 4, 2)
    down = [(int(device[l + 1, x, 0]), int(device[l, x, 0])) for l in range(63) for x in range(4)]
    up = [(int(device[l, x, 1]), int(device[l + 1, x, 1])) for l in range(63) for x in range(4)]
    everyone = LAG + PAR
    raw_next = lax.ppermute(raw, everyone, down)
    prior_last = lax.ppermute(prior, everyone, up)

    zero = call(tile_zero_kernel, shape(2, 4, 64, 512), prior, raw)
    zero = call(add_kernel, shape(4, 64, 512), exchange(zero, "core"))
    zero = call(add_kernel, shape(64, 512), exchange(zero, "x"))
    zero = exchange(zero.reshape(4, 16, 512), "y")

    raw_next, prior_last, zero = lax.optimization_barrier((raw_next, prior_last, zero))
    one = call(tile_one_kernel, shape(4, 4, 2, 16, 512), prior, raw_next, prior_last, raw)
    one = exchange(one.reshape(32, 16, 512), ("y", "x", "core")).reshape(4, 4, 2, 16, 512)

    local, ahead = call(local_prefix_kernel, (shape(4, 2, 16, 512), shape(16, 16, 128)), zero, one)
    back = call(lag_scan_kernel, shape(16, 16, 128), exchange(ahead, "z"))
    rows = call(finish_kernel, shape(4, 32, 512), local, exchange(back, "z"))
    return tuple(call(split_kernel, (shape(1, 64, 512), shape(1, 64, 512)), exchange(rows, "y")))


def solution(mesh):
    chips = Mesh(mesh.devices.reshape(16, 4, 4, 2), LAG + PAR)
    in_specs = (P(LAG, None, PAR), P(LAG, None, PAR))
    out_specs = (P(LAG, PAR, None), P(LAG, PAR, None))
    return jax.shard_map(body, mesh=chips, in_specs=in_specs, out_specs=out_specs, check_vma=False)
```

time: 409 us -> 148 us (0.36)
  the two profiles are of different devices: /device:TPU:504 before, /device:TPU:32 now
where the time goes in v1:
time: 148 us; the launch traced here: 147 us
  blocking collectives  113 us (76%)
  Pallas kernels  27 us (18%)
  starting transfers between devices  5.27 us (4%)
    all_to_all x7, blocking collectives, exchange(): return lax.all_to_all(value, axes, 0, 0, tiled=True)  113 us
    pallas_call x8, Pallas kernels, call(): pl.pallas_call(kernel, out_shape=out_shape, in_specs=[VMEM] * len(args),...  27 us
    ppermute x1, starting transfers between devices, body(): raw_next = lax.ppermute(raw, everyone, down)  4.47 us
  transfers between devices with their start and end apart: 2, of which 0 were waited for; matrix products, arithmetic and copies ran while one was open for 0% of the time, Pallas kernels for 7%

profile of v1, /device:TPU:32, one launch (start us, length us, event | category | flops | bytes accessed | tf_op | source)
XLA Modules:
  0.0 146.8 jit_solution(17616421860547405921)
XLA Ops:
  0.6 0.8 collective-permute-start.1
  1.4 4.5 %collective-permute-start = (bf16[512,2048]{1,0:T(8,128)(2,1)}, bf16[512,2048]{1,0:T(8,128)(2,1)}, u32[]{:S(2)}, u32[]{:S(2)}) collective-permute-start(bf16[512,2048]{1,0:T(8,128)(2,1)} %bitcast.8), channel_id=1, source_target_pairs={{8,0},{10,2},{12,4},{14,6},{16,8},{18,10},{20,12},{22,14},{24,16},... | collective-permute-start | bytes 6291464 | tf_op jit(solution)/shard_map/ppermute | solution.py:121
  5.9 6.1 %shard_map.41 = f32[2,4,64,512]{3,2,1,0:T(8,128)} custom-call(bf16[512,2048]{1,0:T(8,128)(2,1)} %bitcast.6, bf16[512,2048]{1,0:T(8,128)(2,1)} %bitcast.9), custom_call_target="tpu_custom_call" | custom-call | tf_op jit(solution)/shard_map/pallas_call | solution.py:17
  12.0 6.6 %all_to_all.35.parts = f32[2,4,64,512]{3,2,1,0:T(8,128)} all-to-all(f32[2,4,64,512]{3,2,1,0:T(8,128)} %shard_map.41), channel_id=1, replica_groups=mesh['z'=16,'y'=4,'x'=4,'core'=2] {'core'}, dimensions={0} | all-to-all | bytes 2097152 | tf_op jit(solution)/shard_map/all_to_all | solution.py:112
  18.6 2.1 %shard_map.42 = f32[4,64,512]{2,1,0:T(8,128)} custom-call(f32[2,4,64,512]{3,2,1,0:T(8,128)} %all_to_all.35.parts), custom_call_target="tpu_custom_call" | custom-call | tf_op jit(solution)/shard_map/pallas_call | solution.py:17
  20.7 14.3 %all_to_all.36.parts = f32[4,64,512]{2,1,0:T(8,128)} all-to-all(f32[4,64,512]{2,1,0:T(8,128)} %shard_map.42), channel_id=1, replica_groups=mesh['z'=16,'y'=4,'x'=4,'core'=2] {'x'}, dimensions={0} | all-to-all | bytes 1048576 | tf_op jit(solution)/shard_map/all_to_all | solution.py:112
  34.9 1.7 %shard_map.43 = f32[64,512]{1,0:T(8,128)} custom-call(f32[4,64,512]{2,1,0:T(8,128)} %all_to_all.36.parts), custom_call_target="tpu_custom_call" | custom-call | tf_op jit(solution)/shard_map/pallas_call | solution.py:17
  36.7 10.0 %all_to_all.37.zero = f32[4,16,512]{2,1,0:T(8,128)} all-to-all(f32[4,16,512]{2,1,0:T(8,128)} %bitcast.13), channel_id=1, replica_groups=mesh['z'=16,'y'=4,'x'=4,'core'=2] {'y'}, dimensions={0} | all-to-all | bytes 262144 | tf_op jit(solution)/shard_map/all_to_all | solution.py:112
  46.6 0.0 collective-permute-done.1.prior_last
  46.6 0.0 copy-start
  46.6 0.0 collective-permute-done.raw_next
  46.6 1.3 copy-done
  47.9 10.1 %shard_map.44 = f32[4,4,2,16,512]{4,3,2,1,0:T(8,128)} custom-call(bf16[512,2048]{1,0:T(8,128)(2,1)} %bitcast.7, bf16[512,2048]{1,0:T(8,128)(2,1)} %collective-permute-done.raw_next, bf16[512,2048]{1,0:T(8,128)(2,1)} %copy-done, bf16[512,2048]{1,0:T(8,128)(2,1)} %bitcast.10), custom_call_target="tpu_custom_call" | custom-call | tf_op jit(solution)/shard_map/pallas_call | solution.py:17
  58.0 21.8 %all_to_all.38 = f32[32,16,512]{2,1,0:T(8,128)} all-to-all(f32[32,16,512]{2,1,0:T(8,128)} %bitcast.11), channel_id=1, replica_groups=mesh['z'=16,'y'=4,'x'=4,'core'=2] {'y','x','core'}, dimensions={0} | all-to-all | bytes 2097152 | tf_op jit(solution)/shard_map/all_to_all | solution.py:112
  79.9 2.1 %shard_map.45 = (f32[4,2,16,512]{3,2,1,0:T(8,128)}, f32[16,16,128]{2,1,0:T(8,128)}) custom-call(f32[4,16,512]{2,1,0:T(8,128)} %all_to_all.37.zero, f32[4,4,2,16,512]{4,3,2,1,0:T(8,128)} %bitcast.12), custom_call_target="tpu_custom_call" | custom-call | tf_op jit(solution)/shard_map/pallas_call | solution.py:17
  82.0 29.7 %all_to_all.39.ahead = f32[16,16,128]{2,1,0:T(8,128)} all-to-all(f32[16,16,128]{2,1,0:T(8,128)} %get-tuple-element.11), channel_id=1, replica_groups=mesh['z'=16,'y'=4,'x'=4,'core'=2] {'z'}, dimensions={0} | all-to-all | bytes 262144 | tf_op jit(solution)/shard_map/all_to_all | solution.py:112
  111.7 1.6 %shard_map.46 = f32[16,16,128]{2,1,0:T(8,128)} custom-call(f32[16,16,128]{2,1,0:T(8,128)} %all_to_all.39.ahead), custom_call_target="tpu_custom_call" | custom-call | tf_op jit(solution)/shard_map/pallas_call | solution.py:17
  113.2 19.4 %all_to_all.40.back = f32[16,16,128]{2,1,0:T(8,128)} all-to-all(f32[16,16,128]{2,1,0:T(8,128)} %shard_map.46), channel_id=1, replica_groups=mesh['z'=16,'y'=4,'x'=4,'core'=2] {'z'}, dimensions={0} | all-to-all | bytes 262144 | tf_op jit(solution)/shard_map/all_to_all | solution.py:112
  132.7 1.7 %shard_map.47 = f32[4,32,512]{2,1,0:T(8,128)} custom-call(f32[4,2,16,512]{3,2,1,0:T(8,128)} %get-tuple-element.10.local, f32[16,16,128]{2,1,0:T(8,128)} %all_to_all.40.back), custom_call_target="tpu_custom_call" | custom-call | tf_op jit(solution)/shard_map/pallas_call | solution.py:17
  134.4 10.8 %all_to_all.41.rows = f32[4,32,512]{2,1,0:T(8,128)} all-to-all(f32[4,32,512]{2,1,0:T(8,128)} %shard_map.47), channel_id=1, replica_groups=mesh['z'=16,'y'=4,'x'=4,'core'=2] {'y'}, dimensions={0} | all-to-all | bytes 524288 | tf_op jit(solution)/shard_map/all_to_all | solution.py:112
  145.2 1.7 %shard_map.48 = (f32[1,64,512]{2,1,0:T(8,128)}, f32[1,64,512]{2,1,0:T(8,128)}) custom-call(f32[4,32,512]{2,1,0:T(8,128)} %all_to_all.41.rows), custom_call_target="tpu_custom_call" | custom-call | tf_op jit(solution)/shard_map/pallas_call | solution.py:17
Async XLA Ops:
  0.6 46.0 %collective-permute-start.1 = (bf16[512,2048]{1,0:T(8,128)(2,1)}, bf16[512,2048]{1,0:T(8,128)(2,1)S(1)}, u32[]{:S(2)}, u32[]{:S(2)}) collective-permute-start(bf16[512,2048]{1,0:T(8,128)(2,1)} %bitcast.5), channel_id=1, source_target_pairs={{1,9},{3,11},{5,13},{7,15},{9,17},{11,19},{13,21},{15,23},{17,25},... | collective-permute-start | bytes 6291464 | tf_op jit(solution)/shard_map/ppermute | solution.py:122
  1.4 45.2 %collective-permute-start = (bf16[512,2048]{1,0:T(8,128)(2,1)}, bf16[512,2048]{1,0:T(8,128)(2,1)}, u32[]{:S(2)}, u32[]{:S(2)}) collective-permute-start(bf16[512,2048]{1,0:T(8,128)(2,1)} %bitcast.8), channel_id=1, source_target_pairs={{8,0},{10,2},{12,4},{14,6},{16,8},{18,10},{20,12},{22,14},{24,16},... | collective-permute-start | bytes 6291464 | tf_op jit(solution)/shard_map/ppermute | solution.py:121
  46.6 1.3 copy-start

commit v2 on v1

--- a/solution.py
+++ b/solution.py
@@ -13,35 +13,48 @@
 VMEM = pl.BlockSpec(memory_space=pltpu.VMEM)
 
 
+def near(value):
+    return pltpu.with_memory_space_constraint(value, pltpu.VMEM)
+
+
 def call(kernel, out_shape, *args):
     return pl.pallas_call(
         kernel,
         out_shape=out_shape,
         in_specs=[VMEM] * len(args),
         out_specs=jax.tree.map(lambda _: VMEM, out_shape),
-    )(*args)
+        compiler_params=pltpu.CompilerParams(vmem_limit_bytes=6 * 2**20),
+    )(*[near(arg) for arg in args])
 
 
 def shape(*dims):
+    return pltpu.VMEM(dims, F32)
+
+
+def result(*dims):
     return jax.ShapeDtypeStruct(dims, F32)
 
 
 def tile_zero_kernel(prior, raw, out):
+    tile = lax.dot_general(prior[...], raw[...], NT, preferred_element_type=F32)
     for x in range(4):
-        part = lax.dot_general(prior[x * 128 : (x + 1) * 128], raw[...], NT, preferred_element_type=F32)
         for c in range(2):
-            out[c, x] = part[c * 64 : (c + 1) * 64]
+            first = x * 128 + c * 64
+            out[c, x] = tile[first : first + 64]
 
 
 def tile_one_kernel(prior, raw_next, prior_last, raw, out):
-    for x in range(4):
-        rows = slice(x * 128, (x + 1) * 128)
-        part = lax.dot_general(prior[rows], raw_next[...], NT, preferred_element_type=F32)
-        part += lax.dot_general(prior_last[rows], raw[...], NT, preferred_element_type=F32)
-        for c in range(2):
-            for y in range(4):
-                first = c * 64 + y * 16
-                out[y, x, c] = part[first : first + 16]
+    def form(left, right):
+        tile = lax.dot_general(left[...], right[...], NT, preferred_element_type=F32)
+        for x in range(4):
+            for c in range(2):
+                for y in range(4):
+                    first = x * 128 + c * 64 + y * 16
+                    out[y, x, c] = tile[first : first + 16]
+
+    core = lax.axis_index("core")
+    pl.when(core == 0)(lambda: form(prior, raw_next))
+    pl.when(core == 1)(lambda: form(prior_last, raw))
 
 
 def add_kernel(parts, out):
@@ -133,7 +146,7 @@
     local, ahead = call(local_prefix_kernel, (shape(4, 2, 16, 512), shape(16, 16, 128)), zero, one)
     back = call(lag_scan_kernel, shape(16, 16, 128), exchange(ahead, "z"))
     rows = call(finish_kernel, shape(4, 32, 512), local, exchange(back, "z"))
-    return tuple(call(split_kernel, (shape(1, 64, 512), shape(1, 64, 512)), exchange(rows, "y")))
+    return tuple(call(split_kernel, (result(1, 64, 512), result(1, 64, 512)), exchange(rows, "y")))
 
 
 def solution(mesh):

time: 148 us -> 118 us (0.80)
  Pallas kernels: 27 us -> 3.47 us
  blocking collectives: 113 us -> 105 us
  local copies, waits for them, and re-layouts: 1.3 us -> 3.18 us
    pallas_call x8, Pallas kernels: 27 us -> 3.47 us  [call(): pl.pallas_call(kernel, out_shape=out_shape, in_specs=[VMEM] * len(args),...]
    all_to_all x7, blocking collectives: 113 us -> 105 us  [exchange(): return lax.all_to_all(value, axes, 0, 0, tiled=True)]
    unnamed x2 -> x6, local copies, waits for them, and re-layouts: 1.3 us -> 3.18 us
  transfers between devices with their start and end apart: 2 -> 2, of which waited for: 0 -> 0; matrix products, arithmetic and copies ran while one was open for 0% -> 0% of each run, Pallas kernels for 7% -> 1%
where the time goes in v2:
time: 118 us
  blocking collectives  105 us (89%)
  starting transfers between devices  5.26 us (4%)
  Pallas kernels  3.47 us (3%)
  local copies, waits for them, and re-layouts  3.18 us (3%)
    all_to_all x7, blocking collectives, exchange(): return lax.all_to_all(value, axes, 0, 0, tiled=True)  105 us
    ppermute x1, starting transfers between devices, body(): raw_next = lax.ppermute(raw, everyone, down)  4.47 us
    pallas_call x8, Pallas kernels, call(): pl.pallas_call(kernel, out_shape=out_shape, in_specs=[VMEM] * len(args),...  3.47 us
    unnamed x6, local copies, waits for them, and re-layouts  3.18 us
  transfers between devices with their start and end apart: 2, of which 0 were waited for; matrix products, arithmetic and copies ran while one was open for 0% of the time, Pallas kernels for 1%

profile of v2, /device:TPU:32, one launch (start us, length us, event | category | flops | bytes accessed | tf_op | source)
XLA Modules:
  0.0 117.6 jit_solution(5843246521799605095)
XLA Ops:
  0.6 0.8 collective-permute-start.1
  1.4 4.5 %collective-permute-start = (bf16[512,2048]{1,0:T(8,128)(2,1)}, bf16[512,2048]{1,0:T(8,128)(2,1)S(1)}, u32[]{:S(2)}, u32[]{:S(2)}) collective-permute-start(bf16[512,2048]{1,0:T(8,128)(2,1)} %bitcast.8), channel_id=1, source_target_pairs={{8,0},{10,2},{12,4},{14,6},{16,8},{18,10},{20,12},{22,14},{24,16},... | collective-permute-start | bytes 6291464 | tf_op jit(solution)/shard_map/ppermute | solution.py:134
  5.9 0.0 copy-start
  5.9 1.6 %copy-done = bf16[1,512,2048]{2,1,0:T(8,128)(2,1)S(1)} copy-done((bf16[1,512,2048]{2,1,0:T(8,128)(2,1)S(1)}, bf16[1,512,2048]{2,1,0:T(8,128)(2,1)}, u32[]{:S(2)}) %copy-start) | copy-done | bytes 2097176
  7.5 0.0 copy-start.2
  7.5 1.6 %copy-done.2 = bf16[1,512,2048]{2,1,0:T(8,128)(2,1)S(1)} copy-done((bf16[1,512,2048]{2,1,0:T(8,128)(2,1)S(1)}, bf16[1,512,2048]{2,1,0:T(8,128)(2,1)}, u32[]{:S(2)}) %copy-start.2) | copy-done | bytes 2097176
  9.1 1.3 %shard_map.41 = f32[2,4,64,512]{3,2,1,0:T(8,128)S(1)} custom-call(bf16[512,2048]{1,0:T(8,128)(2,1)S(1)} %bitcast.6, bf16[512,2048]{1,0:T(8,128)(2,1)S(1)} %bitcast.9), custom_call_target="tpu_custom_call" | custom-call | tf_op jit(solution)/shard_map/pallas_call | solution.py:21
  10.4 4.6 %all_to_all.35.parts = f32[2,4,64,512]{3,2,1,0:T(8,128)S(1)} all-to-all(f32[2,4,64,512]{3,2,1,0:T(8,128)S(1)} %shard_map.41), channel_id=1, replica_groups=mesh['z'=16,'y'=4,'x'=4,'core'=2] {'core'}, dimensions={0} | all-to-all | bytes 2097152 | tf_op jit(solution)/shard_map/all_to_all | solution.py:125
  15.0 0.0 copy-start.1
  15.0 0.1 shard_map.42
  15.0 14.0 %all_to_all.36.parts = f32[4,64,512]{2,1,0:T(8,128)S(1)} all-to-all(f32[4,64,512]{2,1,0:T(8,128)S(1)} %shard_map.42), channel_id=1, replica_groups=mesh['z'=16,'y'=4,'x'=4,'core'=2] {'x'}, dimensions={0} | all-to-all | bytes 1048576 | tf_op jit(solution)/shard_map/all_to_all | solution.py:125
  29.0 8.4 %all_to_all.37.zero = f32[4,16,512]{2,1,0:T(8,128)S(1)} all-to-all(f32[4,16,512]{2,1,0:T(8,128)S(1)} %bitcast.13), channel_id=1, replica_groups=mesh['z'=16,'y'=4,'x'=4,'core'=2] {'y'}, dimensions={0} | all-to-all | bytes 262144 | tf_op jit(solution)/shard_map/all_to_all | solution.py:125
  37.4 0.0 collective-permute-done.1.prior_last
  37.4 0.0 collective-permute-done.raw_next
  37.4 0.0 copy-done.1
  37.4 1.3 %shard_map.44 = f32[4,4,2,16,512]{4,3,2,1,0:T(8,128)S(1)} custom-call(bf16[512,2048]{1,0:T(8,128)(2,1)S(1)} %bitcast.7, bf16[512,2048]{1,0:T(8,128)(2,1)S(1)} %collective-permute-done.raw_next, bf16[512,2048]{1,0:T(8,128)(2,1)S(1)} %collective-permute-done.1.prior_last, bf16[512,2048]{1,0:T(8,128)(2,1)S(1)} %bitcast.10), custom_call_target="tpu_custom_call" | custom-call | tf_op jit(solution)/shard_map/pallas_call | solution.py:21
  38.7 20.4 %all_to_all.38 = f32[32,16,512]{2,1,0:T(8,128)S(1)} all-to-all(f32[32,16,512]{2,1,0:T(8,128)S(1)} %bitcast.11), channel_id=1, replica_groups=mesh['z'=16,'y'=4,'x'=4,'core'=2] {'y','x','core'}, dimensions={0} | all-to-all | bytes 2097152 | tf_op jit(solution)/shard_map/all_to_all | solution.py:125
  59.2 0.1 shard_map.45
  59.2 29.4 %all_to_all.39.ahead = f32[16,16,128]{2,1,0:T(8,128)S(1)} all-to-all(f32[16,16,128]{2,1,0:T(8,128)S(1)} %get-tuple-element.11), channel_id=1, replica_groups=mesh['z'=16,'y'=4,'x'=4,'core'=2] {'z'}, dimensions={0} | all-to-all | bytes 262144 | tf_op jit(solution)/shard_map/all_to_all | solution.py:125
  88.6 19.1 %all_to_all.40.back = f32[16,16,128]{2,1,0:T(8,128)S(1)} all-to-all(f32[16,16,128]{2,1,0:T(8,128)S(1)} %shard_map.46), channel_id=1, replica_groups=mesh['z'=16,'y'=4,'x'=4,'core'=2] {'z'}, dimensions={0} | all-to-all | bytes 262144 | tf_op jit(solution)/shard_map/all_to_all | solution.py:125
  107.8 9.1 %all_to_all.41.rows = f32[4,32,512]{2,1,0:T(8,128)S(1)} all-to-all(f32[4,32,512]{2,1,0:T(8,128)S(1)} %shard_map.47), channel_id=1, replica_groups=mesh['z'=16,'y'=4,'x'=4,'core'=2] {'y'}, dimensions={0} | all-to-all | bytes 524288 | tf_op jit(solution)/shard_map/all_to_all | solution.py:125
  116.9 0.7 shard_map.48
  (3 shorter events, 0.1 us)
Async XLA Ops:
  0.6 36.8 %collective-permute-start.1 = (bf16[512,2048]{1,0:T(8,128)(2,1)}, bf16[512,2048]{1,0:T(8,128)(2,1)S(1)}, u32[]{:S(2)}, u32[]{:S(2)}) collective-permute-start(bf16[512,2048]{1,0:T(8,128)(2,1)} %bitcast.5), channel_id=1, source_target_pairs={{1,9},{3,11},{5,13},{7,15},{9,17},{11,19},{13,21},{15,23},{17,25},... | collective-permute-start | bytes 6291464 | tf_op jit(solution)/shard_map/ppermute | solution.py:135
  1.4 36.0 %collective-permute-start = (bf16[512,2048]{1,0:T(8,128)(2,1)}, bf16[512,2048]{1,0:T(8,128)(2,1)S(1)}, u32[]{:S(2)}, u32[]{:S(2)}) collective-permute-start(bf16[512,2048]{1,0:T(8,128)(2,1)} %bitcast.8), channel_id=1, source_target_pairs={{8,0},{10,2},{12,4},{14,6},{16,8},{18,10},{20,12},{22,14},{24,16},... | collective-permute-start | bytes 6291464 | tf_op jit(solution)/shard_map/ppermute | solution.py:134
  5.9 1.6 %copy-start = (bf16[1,512,2048]{2,1,0:T(8,128)(2,1)S(1)}, bf16[1,512,2048]{2,1,0:T(8,128)(2,1)}, u32[]{:S(2)}) copy-start(bf16[1,512,2048]{2,1,0:T(8,128)(2,1)} %param.2) | copy-start | bytes 6291460
  7.5 1.6 %copy-start.2 = (bf16[1,512,2048]{2,1,0:T(8,128)(2,1)S(1)}, bf16[1,512,2048]{2,1,0:T(8,128)(2,1)}, u32[]{:S(2)}) copy-start(bf16[1,512,2048]{2,1,0:T(8,128)(2,1)} %param.3) | copy-start | bytes 6291460
  15.0 22.5 %copy-start.1 = (bf16[1,512,2048]{2,1,0:T(8,128)(2,1)S(1)}, bf16[1,512,2048]{2,1,0:T(8,128)(2,1)}, u32[]{:S(2)}) copy-start(bf16[1,512,2048]{2,1,0:T(8,128)(2,1)} %param.2) | copy-start | bytes 6291460

commit v3 on v2

--- a/solution.py
+++ b/solution.py
@@ -7,6 +7,7 @@
 from jax.sharding import Mesh, PartitionSpec as P
 
 F32 = jnp.float32
+F16 = jnp.float16
 NT = (((1,), (1,)), ((), ()))
 LAG = ("z", "y")
 PAR = ("x", "core")
@@ -35,6 +36,24 @@
     return jax.ShapeDtypeStruct(dims, F32)
 
 
+def exponent_of(value):
+    top = jnp.max(jnp.max(jnp.abs(value), axis=0, keepdims=True), axis=1, keepdims=True)
+    return jnp.floor(jnp.log2(jnp.maximum(top, 1e-30)))
+
+
+def pack(value, scale, exponent):
+    half = value.shape[0] // 2
+    sent = value * scale
+    tail = jnp.broadcast_to(exponent, (half, 128))
+    return jnp.concatenate([sent[:half], sent[half:], tail], axis=1)
+
+
+def unpack(sent):
+    scale = jnp.exp2(sent[:, 1024:] - 14.0)
+    scale = jnp.concatenate([scale] * 4, axis=1)
+    return sent[:, :512] * scale, sent[:, 512:1024] * scale
+
+
 def tile_zero_kernel(prior, raw, out):
     tile = lax.dot_general(prior[...], raw[...], NT, preferred_element_type=F32)
     for x in range(4):
@@ -46,22 +65,28 @@
 def tile_one_kernel(prior, raw_next, prior_last, raw, out):
     def form(left, right):
         tile = lax.dot_general(left[...], right[...], NT, preferred_element_type=F32)
+        exponent = exponent_of(tile)
+        scale = jnp.exp2(14.0 - exponent)
         for x in range(4):
             for c in range(2):
                 for y in range(4):
                     first = x * 128 + c * 64 + y * 16
-                    out[y, x, c] = tile[first : first + 16]
+                    out[y, x, c] = pack(tile[first : first + 16], scale, exponent)
 
     core = lax.axis_index("core")
     pl.when(core == 0)(lambda: form(prior, raw_next))
     pl.when(core == 1)(lambda: form(prior_last, raw))
 
 
-def add_kernel(parts, out):
-    total = parts[0]
-    for i in range(1, parts.shape[0]):
-        total = total + parts[i]
-    out[...] = total
+def add_cores_kernel(parts, out):
+    for x in range(4):
+        total = parts[0, x] + parts[1, x]
+        exponent = exponent_of(total)
+        out[x] = pack(total, jnp.exp2(14.0 - exponent), exponent)
+
+
+def add_chips_kernel(parts, out):
+    out[...] = summed([parts[x] for x in range(4)])
 
 
 def spread(ref, half, value, first):
@@ -79,12 +104,18 @@
     return jnp.concatenate(rows, axis=0)
 
 
+def summed(parts):
+    top, bottom = unpack(parts[0])
+    for part in parts[1:]:
+        more_top, more_bottom = unpack(part)
+        top, bottom = top + more_top, bottom + more_bottom
+    return jnp.concatenate([top, bottom], axis=0)
+
+
 def local_prefix_kernel(zero, one, local, ahead):
     total_zero, total_one, delayed = None, None, []
     for lag in range(4):
-        here, late = one[lag, 0, 0], one[lag, 0, 1]
-        for x in range(1, 4):
-            here, late = here + one[lag, x, 0], late + one[lag, x, 1]
+        here, late = (summed([one[lag, x, c] for x in range(4)]) for c in range(2))
         total_zero = zero[lag] if lag == 0 else total_zero + zero[lag]
         local[lag, 0] = total_zero
         if lag == 0:
@@ -125,6 +156,10 @@
     return lax.all_to_all(value, axes, 0, 0, tiled=True)
 
 
+def exchange_short(value, axes):
+    return exchange(value.astype(F16), axes).astype(F32)
+
+
 def body(prior_rows, raw_rows):
     prior, raw = prior_rows[0], raw_rows[0]
     device = np.arange(512).reshape(64, 4, 2)
@@ -135,13 +170,13 @@
     prior_last = lax.ppermute(prior, everyone, up)
 
     zero = call(tile_zero_kernel, shape(2, 4, 64, 512), prior, raw)
-    zero = call(add_kernel, shape(4, 64, 512), exchange(zero, "core"))
-    zero = call(add_kernel, shape(64, 512), exchange(zero, "x"))
+    zero = call(add_cores_kernel, shape(4, 32, 1152), exchange(zero, "core"))
+    zero = call(add_chips_kernel, shape(64, 512), exchange_short(zero, "x"))
     zero = exchange(zero.reshape(4, 16, 512), "y")
 
     raw_next, prior_last, zero = lax.optimization_barrier((raw_next, prior_last, zero))
-    one = call(tile_one_kernel, shape(4, 4, 2, 16, 512), prior, raw_next, prior_last, raw)
-    one = exchange(one.reshape(32, 16, 512), ("y", "x", "core")).reshape(4, 4, 2, 16, 512)
+    one = call(tile_one_kernel, shape(4, 4, 2, 8, 1152), prior, raw_next, prior_last, raw)
+    one = exchange_short(one.reshape(32, 8, 1152), ("y", "x", "core")).reshape(4, 4, 2, 8, 1152)
 
     local, ahead = call(local_prefix_kernel, (shape(4, 2, 16, 512), shape(16, 16, 128)), zero, one)
     back = call(lag_scan_kernel, shape(16, 16, 128), exchange(ahead, "z"))

time: 118 us -> 112 us (0.949)
  the two profiles are of different devices: /device:TPU:32 before, /device:TPU:2 now
where the time goes in v3:
time: 112 us
  blocking collectives  102 us (91%)
  Pallas kernels  3.81 us (3%)
  local copies, waits for them, and re-layouts  3.18 us (3%)
  starting transfers between devices  2.09 us (2%)
    all_to_all x7, blocking collectives, exchange(): return lax.all_to_all(value, axes, 0, 0, tiled=True)  102 us
    pallas_call x8, Pallas kernels, call(): pl.pallas_call(kernel, out_shape=out_shape, in_specs=[VMEM] * len(args),...  3.81 us
    unnamed x8, local copies, waits for them, and re-layouts  3.18 us
  transfers between devices with their start and end apart: 2, of which 0 were waited for; matrix products, arithmetic and copies ran while one was open for 0% of the time, Pallas kernels for 1%

profile of v3, /device:TPU:2, one launch (start us, length us, event | category | flops | bytes accessed | tf_op | source)
XLA Modules:
  0.0 111.8 jit_solution(13305177050218033957)
XLA Ops:
  0.6 0.8 collective-permute-start.1
  1.4 1.3 %collective-permute-start = (bf16[512,2048]{1,0:T(8,128)(2,1)}, bf16[512,2048]{1,0:T(8,128)(2,1)S(1)}, u32[]{:S(2)}, u32[]{:S(2)}) collective-permute-start(bf16[512,2048]{1,0:T(8,128)(2,1)} %bitcast.9), channel_id=1, source_target_pairs={{8,0},{10,2},{12,4},{14,6},{16,8},{18,10},{20,12},{22,14},{24,16},... | collective-permute-start | bytes 6291464 | tf_op jit(solution)/shard_map/ppermute | solution.py:169
  2.7 0.0 copy-start
  2.7 1.6 %copy-done = bf16[1,512,2048]{2,1,0:T(8,128)(2,1)S(1)} copy-done((bf16[1,512,2048]{2,1,0:T(8,128)(2,1)S(1)}, bf16[1,512,2048]{2,1,0:T(8,128)(2,1)}, u32[]{:S(2)}) %copy-start) | copy-done | bytes 2097176
  4.3 0.0 copy-start.2
  4.3 1.6 %copy-done.2 = bf16[1,512,2048]{2,1,0:T(8,128)(2,1)S(1)} copy-done((bf16[1,512,2048]{2,1,0:T(8,128)(2,1)S(1)}, bf16[1,512,2048]{2,1,0:T(8,128)(2,1)}, u32[]{:S(2)}) %copy-start.2) | copy-done | bytes 2097176
  5.9 1.3 %shard_map.41 = f32[2,4,64,512]{3,2,1,0:T(8,128)S(1)} custom-call(bf16[512,2048]{1,0:T(8,128)(2,1)S(1)} %bitcast.7, bf16[512,2048]{1,0:T(8,128)(2,1)S(1)} %bitcast.10), custom_call_target="tpu_custom_call" | custom-call | tf_op jit(solution)/shard_map/pallas_call | solution.py:22
  7.2 5.9 %all_to_all.35.parts = f32[2,4,64,512]{3,2,1,0:T(8,128)S(1)} all-to-all(f32[2,4,64,512]{3,2,1,0:T(8,128)S(1)} %shard_map.41), channel_id=1, replica_groups=mesh['z'=16,'y'=4,'x'=4,'core'=2] {'core'}, dimensions={0} | all-to-all | bytes 2097152 | tf_op jit(solution)/shard_map/all_to_all | solution.py:156
  13.2 0.0 copy-start.1
  13.2 0.0 copy-start.3
  13.2 0.2 shard_map.42
  13.4 13.3 %all_to_all.36 = f16[4,32,1152]{2,1,0:T(8,128)(2,1)S(1)} all-to-all(f16[4,32,1152]{2,1,0:T(8,128)(2,1)S(1)} %convert_element_type.13), channel_id=1, replica_groups=mesh['z'=16,'y'=4,'x'=4,'core'=2] {'x'}, dimensions={0} | all-to-all | bytes 589824 | tf_op jit(solution)/shard_map/all_to_all | solution.py:156
  26.7 9.7 %all_to_all.37.zero = f32[4,16,512]{2,1,0:T(8,128)S(1)} all-to-all(f32[4,16,512]{2,1,0:T(8,128)S(1)} %bitcast.12), channel_id=1, replica_groups=mesh['z'=16,'y'=4,'x'=4,'core'=2] {'y'}, dimensions={0} | all-to-all | bytes 262144 | tf_op jit(solution)/shard_map/all_to_all | solution.py:156
  36.4 0.0 collective-permute-done.1.prior_last
  36.4 0.0 collective-permute-done.raw_next
  36.4 0.0 copy-done.1
  36.4 0.0 copy-done.3
  36.4 1.5 %shard_map.44 = f32[4,4,2,8,1152]{4,3,2,1,0:T(8,128)S(1)} custom-call(bf16[512,2048]{1,0:T(8,128)(2,1)S(1)} %bitcast.8, bf16[512,2048]{1,0:T(8,128)(2,1)S(1)} %collective-permute-done.raw_next, bf16[512,2048]{1,0:T(8,128)(2,1)S(1)} %collective-permute-done.1.prior_last, bf16[512,2048]{1,0:T(8,128)(2,1)S(1)} %bitcast.11), custom_call_target="tpu_custom_call" | custom-call | tf_op jit(solution)/shard_map/pallas_call | solution.py:22
  37.9 0.1 convert_element_type.15
  38.0 15.5 %all_to_all.38 = f16[32,8,1152]{2,1,0:T(8,128)(2,1)S(1)} all-to-all(f16[32,8,1152]{2,1,0:T(8,128)(2,1)S(1)} %bitcast.13), channel_id=1, replica_groups=mesh['z'=16,'y'=4,'x'=4,'core'=2] {'y','x','core'}, dimensions={0} | all-to-all | bytes 1179648 | tf_op jit(solution)/shard_map/all_to_all | solution.py:156
  53.5 0.1 convert.1.one
  53.6 0.1 shard_map.45
  53.7 28.9 %all_to_all.39.ahead = f32[16,16,128]{2,1,0:T(8,128)S(1)} all-to-all(f32[16,16,128]{2,1,0:T(8,128)S(1)} %get-tuple-element.11), channel_id=1, replica_groups=mesh['z'=16,'y'=4,'x'=4,'core'=2] {'z'}, dimensions={0} | all-to-all | bytes 262144 | tf_op jit(solution)/shard_map/all_to_all | solution.py:156
  82.7 19.2 %all_to_all.40.back = f32[16,16,128]{2,1,0:T(8,128)S(1)} all-to-all(f32[16,16,128]{2,1,0:T(8,128)S(1)} %shard_map.46), channel_id=1, replica_groups=mesh['z'=16,'y'=4,'x'=4,'core'=2] {'z'}, dimensions={0} | all-to-all | bytes 262144 | tf_op jit(solution)/shard_map/all_to_all | solution.py:156
  102.0 9.1 %all_to_all.41.rows = f32[4,32,512]{2,1,0:T(8,128)S(1)} all-to-all(f32[4,32,512]{2,1,0:T(8,128)S(1)} %shard_map.47), channel_id=1, replica_groups=mesh['z'=16,'y'=4,'x'=4,'core'=2] {'y'}, dimensions={0} | all-to-all | bytes 524288 | tf_op jit(solution)/shard_map/all_to_all | solution.py:156
  111.0 0.7 shard_map.48
  (5 shorter events, 0.2 us)
Async XLA Ops:
  0.6 35.8 %collective-permute-start.1 = (bf16[512,2048]{1,0:T(8,128)(2,1)}, bf16[512,2048]{1,0:T(8,128)(2,1)S(1)}, u32[]{:S(2)}, u32[]{:S(2)}) collective-permute-start(bf16[512,2048]{1,0:T(8,128)(2,1)} %bitcast.6), channel_id=1, source_target_pairs={{1,9},{3,11},{5,13},{7,15},{9,17},{11,19},{13,21},{15,23},{17,25},... | collective-permute-start | bytes 6291464 | tf_op jit(solution)/shard_map/ppermute | solution.py:170
  1.4 35.0 %collective-permute-start = (bf16[512,2048]{1,0:T(8,128)(2,1)}, bf16[512,2048]{1,0:T(8,128)(2,1)S(1)}, u32[]{:S(2)}, u32[]{:S(2)}) collective-permute-start(bf16[512,2048]{1,0:T(8,128)(2,1)} %bitcast.9), channel_id=1, source_target_pairs={{8,0},{10,2},{12,4},{14,6},{16,8},{18,10},{20,12},{22,14},{24,16},... | collective-permute-start | bytes 6291464 | tf_op jit(solution)/shard_map/ppermute | solution.py:169
  2.7 1.6 %copy-start = (bf16[1,512,2048]{2,1,0:T(8,128)(2,1)S(1)}, bf16[1,512,2048]{2,1,0:T(8,128)(2,1)}, u32[]{:S(2)}) copy-start(bf16[1,512,2048]{2,1,0:T(8,128)(2,1)} %param.2) | copy-start | bytes 6291460
  4.3 1.6 %copy-start.2 = (bf16[1,512,2048]{2,1,0:T(8,128)(2,1)S(1)}, bf16[1,512,2048]{2,1,0:T(8,128)(2,1)}, u32[]{:S(2)}) copy-start(bf16[1,512,2048]{2,1,0:T(8,128)(2,1)} %param.3) | copy-start | bytes 6291460
  13.2 23.3 %copy-start.1 = (bf16[1,512,2048]{2,1,0:T(8,128)(2,1)S(1)}, bf16[1,512,2048]{2,1,0:T(8,128)(2,1)}, u32[]{:S(2)}) copy-start(bf16[1,512,2048]{2,1,0:T(8,128)(2,1)} %param.2) | copy-start | bytes 6291460
  13.2 23.3 %copy-start.3 = (bf16[1,512,2048]{2,1,0:T(8,128)(2,1)S(1)}, bf16[1,512,2048]{2,1,0:T(8,128)(2,1)}, u32[]{:S(2)}) copy-start(bf16[1,512,2048]{2,1,0:T(8,128)(2,1)} %param.3) | copy-start | bytes 6291460

commit v4 on v3

v4 whole, which is shorter than its diff:
```python
import jax
import jax.numpy as jnp
import numpy as np
from jax import lax
from jax.experimental import pallas as pl
from jax.experimental.pallas import tpu as pltpu
from jax.sharding import Mesh, PartitionSpec as P

F32 = jnp.float32
F16 = jnp.float16
NT = (((1,), (1,)), ((), ()))
LAG = ("zh", "zl", "y")
PAR = ("x", "core")
VMEM = pl.BlockSpec(memory_space=pltpu.VMEM)
STEPS = 4


def near(value):
    return pltpu.with_memory_space_constraint(value, pltpu.VMEM)


def far(value):
    return pltpu.with_memory_space_constraint(value, pltpu.HBM)


def call(kernel, out_shape, *args):
    return pl.pallas_call(
        kernel,
        out_shape=out_shape,
        in_specs=[VMEM] * len(args),
        out_specs=jax.tree.map(lambda _: VMEM, out_shape),
        compiler_params=pltpu.CompilerParams(vmem_limit_bytes=6 * 2**20),
    )(*[near(arg) for arg in args])


def shape(*dims):
    return pltpu.VMEM(dims, F32)


def result(*dims):
    return jax.ShapeDtypeStruct(dims, F32)


def exponent_of(value):
    top = jnp.max(jnp.max(jnp.abs(value), axis=0, keepdims=True), axis=1, keepdims=True)
    return jnp.floor(jnp.log2(jnp.maximum(top, 1e-30)))


def pack(tile, out):
    exponent = exponent_of(tile)
    tail = jnp.broadcast_to(exponent, (8, 128))
    sent = tile * jnp.exp2(14.0 - exponent)
    for x in range(4):
        for c in range(2):
            for y in range(4):
                first = x * 128 + c * 64 + y * 16
                top, bottom = sent[first : first + 8], sent[first + 8 : first + 16]
                out[y, x, c] = jnp.concatenate([top, bottom, tail], axis=1)


def unpack(sent):
    scale = jnp.exp2(sent[:, 1024:] - 14.0)
    scale = jnp.concatenate([scale] * 4, axis=1)
    return sent[:, :512] * scale, sent[:, 512:1024] * scale


def summed(parts):
    top, bottom = unpack(parts[0])
    for part in parts[1:]:
        more_top, more_bottom = unpack(part)
        top, bottom = top + more_top, bottom + more_bottom
    return jnp.concatenate([top, bottom], axis=0)


def tile_zero_kernel(prior, raw, out, total):
    step = pl.program_id(0)
    part = lax.dot_general(prior[...], raw[...], NT, preferred_element_type=F32)

    @pl.when(step == 0)
    def _():
        total[...] = part

    @pl.when(step > 0)
    def _():
        total[...] += part

    @pl.when(step == STEPS - 1)
    def _():
        pack(total[...], out)


def tile_one_kernel(prior, raw_next, prior_last, raw, out):
    def form(left, right):
        pack(lax.dot_general(left[...], right[...], NT, preferred_element_type=F32), out)

    core = lax.axis_index("core")
    pl.when(core == 0)(lambda: form(prior, raw_next))
    pl.when(core == 1)(lambda: form(prior_last, raw))


def plane_prefix_kernel(zero, one, out):
    def put(first, value):
        for i in range(4):
            out[i, first : first + 16] = value[:, i * 128 : (i + 1) * 128]

    total_zero, total_one = None, None
    for lag in range(4):
        here = summed([zero[lag, x, c] for x in range(4) for c in range(2)])
        total_zero = here if lag == 0 else total_zero + here
        put(lag * 32, total_zero)
        here, late = (summed([one[lag, x, c] for x in range(4)]) for c in range(2))
        if lag == 0:
            put(128, late)
            total_one = here + late
        else:
            put((lag - 1) * 32 + 16, total_one + late)
            total_one = total_one + here + late
    put(3 * 32 + 16, total_one)


def block_prefix_kernel(planes, local, total):
    state = jnp.zeros((32, 128), F32)
    for zl in range(4):
        for lag in range(4):
            here = planes[zl, lag * 32 : (lag + 1) * 32] + state
            local[zl * 4 + lag, 0:16] = here[0:16]
            if lag == 3 and zl < 3:
                local[zl * 4 + lag, 16:32] = here[16:32] + planes[zl + 1, 128:144]
            else:
                local[zl * 4 + lag, 16:32] = here[16:32]
        state = here
    for i in range(4):
        total[i, 0:32] = state
        total[i, 32:48] = planes[0, 128:144]


def finish_kernel(local, total, out):
    place = lax.axis_index("zh")
    earlier, late = jnp.zeros((32, 128), F32), jnp.zeros((16, 128), F32)
    for z in range(4):
        earlier = earlier + jnp.where(z < place, total[z, 0:32], 0.0)
        late = late + jnp.where(z == place + 1, total[z, 32:48], 0.0)
    for i in range(16):
        out[i] = local[i] + earlier
    out[15, 16:32] = local[15, 16:32] + earlier[16:32] + late


def split_kernel(rows, zero, one):
    for zl in range(4):
        for y in range(4):
            here, there = slice(y * 16, (y + 1) * 16), slice(zl * 128, (zl + 1) * 128)
            zero[0, here, there] = rows[zl * 4 + y, 0:16]
            one[0, here, there] = rows[zl * 4 + y, 16:32]


def exchange(value, axes):
    return lax.all_to_all(value, axes, 0, 0, tiled=True)


def reduce_rows(tile):
    tile = exchange(tile.reshape(32, 8, 1152).astype(F16), ("y", "x", "core"))
    return tile.astype(F32).reshape(4, 4, 2, 8, 1152)


def body(prior_rows, raw_rows):
    prior, raw = prior_rows[0], raw_rows[0]
    device = np.arange(512).reshape(64, 4, 2)
    down = [(int(device[l + 1, x, 0]), int(device[l, x, 0])) for l in range(63) for x in range(4)]
    up = [(int(device[l, x, 1]), int(device[l + 1, x, 1])) for l in range(63) for x in range(4)]
    raw_next = lax.ppermute(raw, LAG + PAR, down)
    prior_last = lax.ppermute(prior, LAG + PAR, up)

    sent = shape(4, 4, 2, 8, 1152)
    piece = pl.BlockSpec((512, 2048 // STEPS), lambda step: (0, step))
    zero = pl.pallas_call(
        tile_zero_kernel,
        out_shape=sent,
        grid=(STEPS,),
        in_specs=[piece, piece],
        out_specs=VMEM,
        scratch_shapes=[pltpu.VMEM((512, 512), F32)],
        compiler_params=pltpu.CompilerParams(vmem_limit_bytes=8 * 2**20),
    )(far(prior), far(raw))
    zero = reduce_rows(zero)

    raw_next, prior_last, zero = lax.optimization_barrier((raw_next, prior_last, zero))
    one = reduce_rows(call(tile_one_kernel, sent, prior, raw_next, prior_last, raw))

    planes = exchange(call(plane_prefix_kernel, shape(4, 144, 128), zero, one), "zl")
    local, total = call(block_prefix_kernel, (shape(16, 32, 128), shape(4, 48, 128)), planes)
    rows = call(finish_kernel, shape(16, 32, 128), local, exchange(total, "zh"))
    return tuple(call(split_kernel, (result(1, 64, 512), result(1, 64, 512)), exchange(rows, ("zl", "y"))))


def solution(mesh):
    chips = Mesh(mesh.devices.reshape(4, 4, 4, 4, 2), LAG + PAR)
    in_specs = (P(LAG, None, PAR), P(LAG, None, PAR))
    out_specs = (P(LAG, PAR, None), P(LAG, PAR, None))
    return jax.shard_map(body, mesh=chips, in_specs=in_specs, out_specs=out_specs, check_vma=False)
```

time: 112 us -> 116 us (1.036)
  blocking collectives: 102 us -> 106 us
  local copies, waits for them, and re-layouts: 3.18 us -> 0.01 us
  Pallas kernels: 3.81 us -> 6.82 us
    all_to_all x7 -> x5, blocking collectives: 102 us -> 106 us  [exchange(): return lax.all_to_all(value, axes, 0, 0, tiled=True)]
    pallas_call x0 -> x1, Pallas kernels: none -> 4.41 us  [body(): pl.pallas_call(tile_zero_kernel, out_shape=sent, grid=(STEPS,), in_specs=...]
    unnamed x8 -> x4, local copies, waits for them, and re-layouts: 3.18 us -> 0.01 us
    pallas_call x8 -> x5, Pallas kernels: 3.81 us -> 2.41 us  [call(): pl.pallas_call(kernel, out_shape=out_shape, in_specs=[VMEM] * len(args),...]
  transfers between devices with their start and end apart: 2 -> 2, of which waited for: 0 -> 0; matrix products, arithmetic and copies ran while one was open for 0% -> 0% of each run, Pallas kernels for 1% -> 4%
where the time goes in v4:
time: 116 us
  blocking collectives  106 us (91%)
  Pallas kernels  6.82 us (6%)
  starting transfers between devices  2.09 us (2%)
    all_to_all x5, blocking collectives, exchange(): return lax.all_to_all(value, axes, 0, 0, tiled=True)  106 us
    pallas_call x1, Pallas kernels, body(): pl.pallas_call(tile_zero_kernel, out_shape=sent, grid=(STEPS,), in_specs=...  4.41 us
    pallas_call x5, Pallas kernels, call(): pl.pallas_call(kernel, out_shape=out_shape, in_specs=[VMEM] * len(args),...  2.41 us
  transfers between devices with their start and end apart: 2, of which 0 were waited for; matrix products, arithmetic and copies ran while one was open for 0% of the time, Pallas kernels for 4%

profile of v4, /device:TPU:2, one launch (start us, length us, event | category | flops | bytes accessed | tf_op | source)
XLA Modules:
  0.0 116.1 jit_solution(1447784067032450621)
XLA Ops:
  0.6 0.8 collective-permute-start.1
  1.4 1.3 %collective-permute-start = (bf16[512,2048]{1,0:T(8,128)(2,1)}, bf16[512,2048]{1,0:T(8,128)(2,1)S(1)}, u32[]{:S(2)}, u32[]{:S(2)}) collective-permute-start(bf16[512,2048]{1,0:T(8,128)(2,1)} %bitcast.11), channel_id=1, source_target_pairs={{8,0},{10,2},{12,4},{14,6},{16,8},{18,10},{20,12},{22,14},{24,16},... | collective-permute-start | bytes 6291464 | tf_op jit(solution)/shard_map/ppermute | solution.py:170
  2.7 4.4 %shard_map.41 = f32[4,4,2,8,1152]{4,3,2,1,0:T(8,128)S(1)} custom-call(bf16[512,2048]{1,0:T(8,128)(2,1)} %bitcast.9, bf16[512,2048]{1,0:T(8,128)(2,1)} %bitcast.12), custom_call_target="tpu_custom_call" | custom-call | tf_op jit(solution)/shard_map/pallas_call | solution.py:175
  7.1 0.0 copy-start
  7.2 0.0 copy-start.1
  7.2 0.1 convert_element_type.14
  7.2 30.1 %all_to_all.25 = f16[32,8,1152]{2,1,0:T(8,128)(2,1)S(1)} all-to-all(f16[32,8,1152]{2,1,0:T(8,128)(2,1)S(1)} %bitcast.14), channel_id=1, replica_groups=mesh['zh'=4,'zl'=4,'y'=4,'x'=4,'core'=2] {'y','x','core'}, dimensions={0} | all-to-all | bytes 1179648 | tf_op jit(solution)/shard_map/all_to_all | solution.py:157
  37.4 0.1 convert.2.zero
  37.5 0.0 collective-permute-done.1.prior_last
  37.5 0.0 collective-permute-done.raw_next
  37.5 0.0 copy-done
  37.5 0.0 copy-done.1
  37.5 1.5 %shard_map.42 = f32[4,4,2,8,1152]{4,3,2,1,0:T(8,128)S(1)} custom-call(bf16[512,2048]{1,0:T(8,128)(2,1)S(1)} %bitcast.10, bf16[512,2048]{1,0:T(8,128)(2,1)S(1)} %collective-permute-done.raw_next, bf16[512,2048]{1,0:T(8,128)(2,1)S(1)} %collective-permute-done.1.prior_last, bf16[512,2048]{1,0:T(8,128)(2,1)S(1)} %bitcast.13), custom_call_target="tpu_custom_call" | custom-call | tf_op jit(solution)/shard_map/pallas_call | solution.py:27
  39.0 0.1 convert_element_type.16
  39.0 19.4 %all_to_all.26 = f16[32,8,1152]{2,1,0:T(8,128)(2,1)S(1)} all-to-all(f16[32,8,1152]{2,1,0:T(8,128)(2,1)S(1)} %bitcast.16), channel_id=1, replica_groups=mesh['zh'=4,'zl'=4,'y'=4,'x'=4,'core'=2] {'y','x','core'}, dimensions={0} | all-to-all | bytes 1179648 | tf_op jit(solution)/shard_map/all_to_all | solution.py:157
  58.4 0.1 convert.3.one
  58.5 0.2 shard_map.43
  58.7 16.6 %all_to_all.27.planes = f32[4,144,128]{2,1,0:T(8,128)S(1)} all-to-all(f32[4,144,128]{2,1,0:T(8,128)S(1)} %shard_map.43), channel_id=1, replica_groups=mesh['zh'=4,'zl'=4,'y'=4,'x'=4,'core'=2] {'zl'}, dimensions={0} | all-to-all | bytes 589824 | tf_op jit(solution)/shard_map/all_to_all | solution.py:157
  75.3 25.5 %all_to_all.28.total = f32[4,48,128]{2,1,0:T(8,128)S(1)} all-to-all(f32[4,48,128]{2,1,0:T(8,128)S(1)} %get-tuple-element.11), channel_id=1, replica_groups=mesh['zh'=4,'zl'=4,'y'=4,'x'=4,'core'=2] {'zh'}, dimensions={0} | all-to-all | bytes 196608 | tf_op jit(solution)/shard_map/all_to_all | solution.py:157
  100.9 14.5 %all_to_all.29.rows = f32[16,32,128]{2,1,0:T(8,128)S(1)} all-to-all(f32[16,32,128]{2,1,0:T(8,128)S(1)} %shard_map.45), channel_id=1, replica_groups=mesh['zh'=4,'zl'=4,'y'=4,'x'=4,'core'=2] {'zl','y'}, dimensions={0} | all-to-all | bytes 524288 | tf_op jit(solution)/shard_map/all_to_all | solution.py:157
  115.4 0.7 shard_map.46
  (2 shorter events, 0.1 us)
Async XLA Ops:
  0.6 36.8 %collective-permute-start.1 = (bf16[512,2048]{1,0:T(8,128)(2,1)}, bf16[512,2048]{1,0:T(8,128)(2,1)S(1)}, u32[]{:S(2)}, u32[]{:S(2)}) collective-permute-start(bf16[512,2048]{1,0:T(8,128)(2,1)} %bitcast.8), channel_id=1, source_target_pairs={{1,9},{3,11},{5,13},{7,15},{9,17},{11,19},{13,21},{15,23},{17,25},... | collective-permute-start | bytes 6291464 | tf_op jit(solution)/shard_map/ppermute | solution.py:171
  1.4 36.0 %collective-permute-start = (bf16[512,2048]{1,0:T(8,128)(2,1)}, bf16[512,2048]{1,0:T(8,128)(2,1)S(1)}, u32[]{:S(2)}, u32[]{:S(2)}) collective-permute-start(bf16[512,2048]{1,0:T(8,128)(2,1)} %bitcast.11), channel_id=1, source_target_pairs={{8,0},{10,2},{12,4},{14,6},{16,8},{18,10},{20,12},{22,14},{24,16},... | collective-permute-start | bytes 6291464 | tf_op jit(solution)/shard_map/ppermute | solution.py:170
  7.1 30.3 %copy-start = (bf16[1,512,2048]{2,1,0:T(8,128)(2,1)S(1)}, bf16[1,512,2048]{2,1,0:T(8,128)(2,1)}, u32[]{:S(2)}) copy-start(bf16[1,512,2048]{2,1,0:T(8,128)(2,1)} %param.2) | copy-start | bytes 6291460
  7.2 30.3 %copy-start.1 = (bf16[1,512,2048]{2,1,0:T(8,128)(2,1)S(1)}, bf16[1,512,2048]{2,1,0:T(8,128)(2,1)}, u32[]{:S(2)}) copy-start(bf16[1,512,2048]{2,1,0:T(8,128)(2,1)} %param.3) | copy-start | bytes 6291460

commit v5 on v4

--- a/solution.py
+++ b/solution.py
@@ -52,24 +52,20 @@
     sent = tile * jnp.exp2(14.0 - exponent)
     for x in range(4):
         for c in range(2):
-            for y in range(4):
-                first = x * 128 + c * 64 + y * 16
-                top, bottom = sent[first : first + 8], sent[first + 8 : first + 16]
-                out[y, x, c] = jnp.concatenate([top, bottom, tail], axis=1)
-
-
-def unpack(sent):
-    scale = jnp.exp2(sent[:, 1024:] - 14.0)
-    scale = jnp.concatenate([scale] * 4, axis=1)
-    return sent[:, :512] * scale, sent[:, 512:1024] * scale
+            first = x * 128 + c * 64
+            groups = [sent[first + i * 8 : first + (i + 1) * 8] for i in range(8)]
+            out[x, c] = jnp.concatenate(groups + [tail], axis=1)
 
 
 def summed(parts):
-    top, bottom = unpack(parts[0])
-    for part in parts[1:]:
-        more_top, more_bottom = unpack(part)
-        top, bottom = top + more_top, bottom + more_bottom
-    return jnp.concatenate([top, bottom], axis=0)
+    groups = [None] * 8
+    for part in parts:
+        scale = jnp.exp2(part[:, 4096:] - 14.0)
+        scale = jnp.concatenate([scale] * 4, axis=1)
+        for i in range(8):
+            group = part[:, i * 512 : (i + 1) * 512] * scale
+            groups[i] = group if groups[i] is None else groups[i] + group
+    return jnp.concatenate(groups, axis=0)
 
 
 def tile_zero_kernel(prior, raw, out, total):
@@ -98,40 +94,26 @@
     pl.when(core == 1)(lambda: form(prior_last, raw))
 
 
-def plane_prefix_kernel(zero, one, out):
-    def put(first, value):
-        for i in range(4):
-            out[i, first : first + 16] = value[:, i * 128 : (i + 1) * 128]
-
-    total_zero, total_one = None, None
-    for lag in range(4):
-        here = summed([zero[lag, x, c] for x in range(4) for c in range(2)])
-        total_zero = here if lag == 0 else total_zero + here
-        put(lag * 32, total_zero)
-        here, late = (summed([one[lag, x, c] for x in range(4)]) for c in range(2))
-        if lag == 0:
-            put(128, late)
-            total_one = here + late
-        else:
-            put((lag - 1) * 32 + 16, total_one + late)
-            total_one = total_one + here + late
-    put(3 * 32 + 16, total_one)
+def spread_kernel(zero, one, out):
+    whole = summed([zero[x, c] for x in range(4) for c in range(2)])
+    here, late = (summed([one[x, c] for x in range(4)]) for c in range(2))
+    for i, value in enumerate((whole, here, late)):
+        for zl in range(4):
+            for y in range(4):
+                out[zl * 4 + y, i * 16 : (i + 1) * 16] = value[y * 16 : (y + 1) * 16, zl * 128 : (zl + 1) * 128]
 
 
-def block_prefix_kernel(planes, local, total):
-    state = jnp.zeros((32, 128), F32)
-    for zl in range(4):
-        for lag in range(4):
-            here = planes[zl, lag * 32 : (lag + 1) * 32] + state
-            local[zl * 4 + lag, 0:16] = here[0:16]
-            if lag == 3 and zl < 3:
-                local[zl * 4 + lag, 16:32] = here[16:32] + planes[zl + 1, 128:144]
-            else:
-                local[zl * 4 + lag, 16:32] = here[16:32]
-        state = here
+def block_prefix_kernel(lags, local, total):
+    zero, one = jnp.zeros((16, 128), F32), jnp.zeros((16, 128), F32)
+    for lag in range(16):
+        zero = zero + lags[lag, 0:16]
+        one = one + lags[lag, 16:32] + lags[lag, 32:48]
+        local[lag, 0:16] = zero
+        local[lag, 16:32] = one + lags[lag + 1, 32:48] if lag < 15 else one
     for i in range(4):
-        total[i, 0:32] = state
-        total[i, 32:48] = planes[0, 128:144]
+        total[i, 0:16] = zero
+        total[i, 16:32] = one
+        total[i, 32:48] = lags[0, 32:48]
 
 
 def finish_kernel(local, total, out):
@@ -158,8 +140,8 @@
 
 
 def reduce_rows(tile):
-    tile = exchange(tile.reshape(32, 8, 1152).astype(F16), ("y", "x", "core"))
-    return tile.astype(F32).reshape(4, 4, 2, 8, 1152)
+    tile = exchange(tile.reshape(8, 8, 4224).astype(F16), PAR)
+    return tile.astype(F32).reshape(4, 2, 8, 4224)
 
 
 def body(prior_rows, raw_rows):
@@ -170,7 +152,7 @@
     raw_next = lax.ppermute(raw, LAG + PAR, down)
     prior_last = lax.ppermute(prior, LAG + PAR, up)
 
-    sent = shape(4, 4, 2, 8, 1152)
+    sent = shape(4, 2, 8, 4224)
     piece = pl.BlockSpec((512, 2048 // STEPS), lambda step: (0, step))
     zero = pl.pallas_call(
         tile_zero_kernel,
@@ -186,8 +168,8 @@
     raw_next, prior_last, zero = lax.optimization_barrier((raw_next, prior_last, zero))
     one = reduce_rows(call(tile_one_kernel, sent, prior, raw_next, prior_last, raw))
 
-    planes = exchange(call(plane_prefix_kernel, shape(4, 144, 128), zero, one), "zl")
-    local, total = call(block_prefix_kernel, (shape(16, 32, 128), shape(4, 48, 128)), planes)
+    lags = exchange(call(spread_kernel, shape(16, 48, 128), zero, one), ("zl", "y"))
+    local, total = call(block_prefix_kernel, (shape(16, 32, 128), shape(4, 48, 128)), lags)
     rows = call(finish_kernel, shape(16, 32, 128), local, exchange(total, "zh"))
     return tuple(call(split_kernel, (result(1, 64, 512), result(1, 64, 512)), exchange(rows, ("zl", "y"))))
 

time: 116 us -> 111 us (0.957)
  blocking collectives: 106 us -> 96 us
  waiting for transfers between devices: 0.01 us -> 4.61 us
    all_to_all x5, blocking collectives: 106 us -> 96 us  [exchange(): return lax.all_to_all(value, axes, 0, 0, tiled=True)]
    ppermute x1, waiting for transfers between devices: 0.01 us -> 4.61 us  [body(): raw_next = lax.ppermute(raw, LAG + PAR, down)]
  transfers between devices with their start and end apart: 2 -> 2, of which waited for: 0 -> 1; matrix products, arithmetic and copies ran while one was open for 0% -> 0% of each run, Pallas kernels for 4% -> 4%
where the time goes in v5:
time: 111 us; the launch traced here: 110 us
  blocking collectives  96 us (86%)
  Pallas kernels  6.8 us (6%)
  waiting for transfers between devices  4.61 us (4%)
  starting transfers between devices  2.09 us (2%)
    all_to_all x5, blocking collectives, exchange(): return lax.all_to_all(value, axes, 0, 0, tiled=True)  96 us
    ppermute x1, waiting for transfers between devices, body(): raw_next = lax.ppermute(raw, LAG + PAR, down)  4.61 us
    pallas_call x1, Pallas kernels, body(): pl.pallas_call(tile_zero_kernel, out_shape=sent, grid=(STEPS,), in_specs=...  4.41 us
    pallas_call x5, Pallas kernels, call(): pl.pallas_call(kernel, out_shape=out_shape, in_specs=[VMEM] * len(args),...  2.39 us
  transfers between devices with their start and end apart: 2, of which 1 were waited for; matrix products, arithmetic and copies ran while one was open for 0% of the time, Pallas kernels for 4%

profile of v5, /device:TPU:2, one launch (start us, length us, event | category | flops | bytes accessed | tf_op | source)
XLA Modules:
  0.0 110.5 jit_solution(13057473886073311479)
XLA Ops:
  0.6 0.8 collective-permute-start.1
  1.4 1.3 %collective-permute-start = (bf16[512,2048]{1,0:T(8,128)(2,1)}, bf16[512,2048]{1,0:T(8,128)(2,1)S(1)}, u32[]{:S(2)}, u32[]{:S(2)}) collective-permute-start(bf16[512,2048]{1,0:T(8,128)(2,1)} %bitcast.11), channel_id=1, source_target_pairs={{8,0},{10,2},{12,4},{14,6},{16,8},{18,10},{20,12},{22,14},{24,16},... | collective-permute-start | bytes 6291464 | tf_op jit(solution)/shard_map/ppermute | solution.py:152
  2.7 4.4 %shard_map.41 = f32[4,2,8,4224]{3,2,1,0:T(8,128)S(1)} custom-call(bf16[512,2048]{1,0:T(8,128)(2,1)} %bitcast.9, bf16[512,2048]{1,0:T(8,128)(2,1)} %bitcast.12), custom_call_target="tpu_custom_call" | custom-call | tf_op jit(solution)/shard_map/pallas_call | solution.py:157
  7.1 0.0 copy-start
  7.2 0.0 copy-start.1
  7.2 0.1 convert_element_type.14
  7.2 17.6 %all_to_all.25 = f16[8,8,4224]{2,1,0:T(8,128)(2,1)S(1)} all-to-all(f16[8,8,4224]{2,1,0:T(8,128)(2,1)S(1)} %bitcast.14), channel_id=1, replica_groups=mesh['zh'=4,'zl'=4,'y'=4,'x'=4,'core'=2] {'x','core'}, dimensions={0} | all-to-all | bytes 1081344 | tf_op jit(solution)/shard_map/all_to_all | solution.py:139
  24.9 0.1 convert.2.zero
  24.9 0.0 collective-permute-done.1.prior_last
  25.0 4.6 %collective-permute-done.raw_next = bf16[512,2048]{1,0:T(8,128)(2,1)S(1)} collective-permute-done((bf16[512,2048]{1,0:T(8,128)(2,1)}, bf16[512,2048]{1,0:T(8,128)(2,1)S(1)}, u32[]{:S(2)}, u32[]{:S(2)}) %collective-permute-start) | collective-permute-done | bytes 2097184 | tf_op jit(solution)/shard_map/ppermute | solution.py:152
  29.6 0.0 copy-done
  29.6 0.0 copy-done.1
  29.6 1.5 %shard_map.42 = f32[4,2,8,4224]{3,2,1,0:T(8,128)S(1)} custom-call(bf16[512,2048]{1,0:T(8,128)(2,1)S(1)} %bitcast.10, bf16[512,2048]{1,0:T(8,128)(2,1)S(1)} %collective-permute-done.raw_next, bf16[512,2048]{1,0:T(8,128)(2,1)S(1)} %collective-permute-done.1.prior_last, bf16[512,2048]{1,0:T(8,128)(2,1)S(1)} %bitcast.13), custom_call_target="tpu_custom_call" | custom-call | tf_op jit(solution)/shard_map/pallas_call | solution.py:27
  31.0 0.1 convert_element_type.16
  31.1 17.4 %all_to_all.26 = f16[8,8,4224]{2,1,0:T(8,128)(2,1)S(1)} all-to-all(f16[8,8,4224]{2,1,0:T(8,128)(2,1)S(1)} %bitcast.16), channel_id=1, replica_groups=mesh['zh'=4,'zl'=4,'y'=4,'x'=4,'core'=2] {'x','core'}, dimensions={0} | all-to-all | bytes 1081344 | tf_op jit(solution)/shard_map/all_to_all | solution.py:139
  48.5 0.1 convert.3.one
  48.5 0.1 shard_map.43
  48.7 21.2 %all_to_all.27.lags = f32[16,48,128]{2,1,0:T(8,128)S(1)} all-to-all(f32[16,48,128]{2,1,0:T(8,128)S(1)} %shard_map.43), channel_id=1, replica_groups=mesh['zh'=4,'zl'=4,'y'=4,'x'=4,'core'=2] {'zl','y'}, dimensions={0} | all-to-all | bytes 786432 | tf_op jit(solution)/shard_map/all_to_all | solution.py:139
  70.0 25.8 %all_to_all.28.total = f32[4,48,128]{2,1,0:T(8,128)S(1)} all-to-all(f32[4,48,128]{2,1,0:T(8,128)S(1)} %get-tuple-element.11), channel_id=1, replica_groups=mesh['zh'=4,'zl'=4,'y'=4,'x'=4,'core'=2] {'zh'}, dimensions={0} | all-to-all | bytes 196608 | tf_op jit(solution)/shard_map/all_to_all | solution.py:139
  95.8 13.9 %all_to_all.29.rows = f32[16,32,128]{2,1,0:T(8,128)S(1)} all-to-all(f32[16,32,128]{2,1,0:T(8,128)S(1)} %shard_map.45), channel_id=1, replica_groups=mesh['zh'=4,'zl'=4,'y'=4,'x'=4,'core'=2] {'zl','y'}, dimensions={0} | all-to-all | bytes 524288 | tf_op jit(solution)/shard_map/all_to_all | solution.py:139
  109.7 0.7 shard_map.46
  (2 shorter events, 0.1 us)
Async XLA Ops:
  0.6 24.3 %collective-permute-start.1 = (bf16[512,2048]{1,0:T(8,128)(2,1)}, bf16[512,2048]{1,0:T(8,128)(2,1)S(1)}, u32[]{:S(2)}, u32[]{:S(2)}) collective-permute-start(bf16[512,2048]{1,0:T(8,128)(2,1)} %bitcast.8), channel_id=1, source_target_pairs={{1,9},{3,11},{5,13},{7,15},{9,17},{11,19},{13,21},{15,23},{17,25},... | collective-permute-start | bytes 6291464 | tf_op jit(solution)/shard_map/ppermute | solution.py:153
  1.4 28.1 %collective-permute-start = (bf16[512,2048]{1,0:T(8,128)(2,1)}, bf16[512,2048]{1,0:T(8,128)(2,1)S(1)}, u32[]{:S(2)}, u32[]{:S(2)}) collective-permute-start(bf16[512,2048]{1,0:T(8,128)(2,1)} %bitcast.11), channel_id=1, source_target_pairs={{8,0},{10,2},{12,4},{14,6},{16,8},{18,10},{20,12},{22,14},{24,16},... | collective-permute-start | bytes 6291464 | tf_op jit(solution)/shard_map/ppermute | solution.py:152
  7.1 22.4 %copy-start = (bf16[1,512,2048]{2,1,0:T(8,128)(2,1)S(1)}, bf16[1,512,2048]{2,1,0:T(8,128)(2,1)}, u32[]{:S(2)}) copy-start(bf16[1,512,2048]{2,1,0:T(8,128)(2,1)} %param.2) | copy-start | bytes 6291460
  7.2 22.4 %copy-start.1 = (bf16[1,512,2048]{2,1,0:T(8,128)(2,1)S(1)}, bf16[1,512,2048]{2,1,0:T(8,128)(2,1)}, u32[]{:S(2)}) copy-start(bf16[1,512,2048]{2,1,0:T(8,128)(2,1)} %param.3) | copy-start | bytes 6291460

commit v6 on v5

--- a/solution.py
+++ b/solution.py
@@ -44,6 +44,27 @@
 def exponent_of(value):
     top = jnp.max(jnp.max(jnp.abs(value), axis=0, keepdims=True), axis=1, keepdims=True)
     return jnp.floor(jnp.log2(jnp.maximum(top, 1e-30)))
+
+
+LEVEL = 3.3
+
+
+def encode(value, exponent):
+    size = jnp.abs(value) * jnp.exp2(7.0 - exponent)
+    binade = jnp.floor(jnp.log2(jnp.maximum(size, 1.0)))
+    place = LEVEL * (binade + size * jnp.exp2(-binade))
+    whole = jnp.floor(place)
+    code = jnp.exp2(whole - 14.0) * (1.0 + (place - whole))
+    return jnp.where(value < 0, -code, code)
+
+
+def decode(code, exponent):
+    size = jnp.abs(code)
+    whole = jnp.floor(jnp.log2(jnp.maximum(size, 2.0**-14)))
+    place = (whole + 13.0 + size * jnp.exp2(-whole)) * (1.0 / LEVEL)
+    binade = jnp.maximum(jnp.floor(place) - 1.0, 0.0)
+    value = (place - binade) * jnp.exp2(binade + exponent - 7.0)
+    return jnp.where(code < 0, -value, value)
 
 
 def pack(tile, out):
@@ -98,22 +119,31 @@
     whole = summed([zero[x, c] for x in range(4) for c in range(2)])
     here, late = (summed([one[x, c] for x in range(4)]) for c in range(2))
     for i, value in enumerate((whole, here, late)):
+        exponent = exponent_of(value)
+        value = encode(value, exponent)
         for zl in range(4):
             for y in range(4):
                 out[zl * 4 + y, i * 16 : (i + 1) * 16] = value[y * 16 : (y + 1) * 16, zl * 128 : (zl + 1) * 128]
+                out[zl * 4 + y, 48 + i * 8 : 56 + i * 8] = jnp.broadcast_to(exponent, (8, 128))
 
 
 def block_prefix_kernel(lags, local, total):
+    def read(lag, i):
+        exponent = lags[lag, 48 + i * 8 : 56 + i * 8]
+        exponent = jnp.concatenate([exponent, exponent], axis=0)
+        return decode(lags[lag, i * 16 : (i + 1) * 16], exponent)
+
     zero, one = jnp.zeros((16, 128), F32), jnp.zeros((16, 128), F32)
+    lates = [read(lag, 2) for lag in range(16)]
     for lag in range(16):
-        zero = zero + lags[lag, 0:16]
-        one = one + lags[lag, 16:32] + lags[lag, 32:48]
+        zero = zero + read(lag, 0)
+        one = one + read(lag, 1) + lates[lag]
         local[lag, 0:16] = zero
-        local[lag, 16:32] = one + lags[lag + 1, 32:48] if lag < 15 else one
+        local[lag, 16:32] = one + lates[lag + 1] if lag < 15 else one
     for i in range(4):
         total[i, 0:16] = zero
         total[i, 16:32] = one
-        total[i, 32:48] = lags[0, 32:48]
+        total[i, 32:48] = lates[0]
 
 
 def finish_kernel(local, total, out):
@@ -122,26 +152,37 @@
     for z in range(4):
         earlier = earlier + jnp.where(z < place, total[z, 0:32], 0.0)
         late = late + jnp.where(z == place + 1, total[z, 32:48], 0.0)
-    for i in range(16):
-        out[i] = local[i] + earlier
-    out[15, 16:32] = local[15, 16:32] + earlier[16:32] + late
+    rows = [local[i] + earlier for i in range(16)]
+    rows[15] = jnp.concatenate([rows[15][0:16], rows[15][16:32] + late], axis=0)
+    for i in range(2):
+        part = jnp.concatenate([row[i * 16 : (i + 1) * 16] for row in rows], axis=0)
+        exponent = exponent_of(part)
+        part = encode(part, exponent)
+        for lag in range(16):
+            out[lag, i * 16 : (i + 1) * 16] = part[lag * 16 : (lag + 1) * 16]
+            out[lag, 32 + i * 8 : 40 + i * 8] = jnp.broadcast_to(exponent, (8, 128))
 
 
 def split_kernel(rows, zero, one):
     for zl in range(4):
         for y in range(4):
             here, there = slice(y * 16, (y + 1) * 16), slice(zl * 128, (zl + 1) * 128)
-            zero[0, here, there] = rows[zl * 4 + y, 0:16]
-            one[0, here, there] = rows[zl * 4 + y, 16:32]
+            for i, out in enumerate((zero, one)):
+                exponent = rows[zl * 4 + y, 32 + i * 8 : 40 + i * 8]
+                exponent = jnp.concatenate([exponent, exponent], axis=0)
+                out[0, here, there] = decode(rows[zl * 4 + y, i * 16 : (i + 1) * 16], exponent)
 
 
 def exchange(value, axes):
     return lax.all_to_all(value, axes, 0, 0, tiled=True)
 
 
+def exchange_short(value, axes):
+    return exchange(value.astype(F16), axes).astype(F32)
+
+
 def reduce_rows(tile):
-    tile = exchange(tile.reshape(8, 8, 4224).astype(F16), PAR)
-    return tile.astype(F32).reshape(4, 2, 8, 4224)
+    return exchange_short(tile.reshape(8, 8, 4224), PAR).reshape(4, 2, 8, 4224)
 
 
 def body(prior_rows, raw_rows):
@@ -168,10 +209,11 @@
     raw_next, prior_last, zero = lax.optimization_barrier((raw_next, prior_last, zero))
     one = reduce_rows(call(tile_one_kernel, sent, prior, raw_next, prior_last, raw))
 
-    lags = exchange(call(spread_kernel, shape(16, 48, 128), zero, one), ("zl", "y"))
+    lags = exchange_short(call(spread_kernel, shape(16, 72, 128), zero, one), ("zl", "y"))
     local, total = call(block_prefix_kernel, (shape(16, 32, 128), shape(4, 48, 128)), lags)
-    rows = call(finish_kernel, shape(16, 32, 128), local, exchange(total, "zh"))
-    return tuple(call(split_kernel, (result(1, 64, 512), result(1, 64, 512)), exchange(rows, ("zl", "y"))))
+    rows = call(finish_kernel, shape(16, 48, 128), local, exchange(total, "zh"))
+    rows = exchange_short(rows, ("zl", "y"))
+    return tuple(call(split_kernel, (result(1, 64, 512), result(1, 64, 512)), rows))
 
 
 def solution(mesh):

time: 111 us -> 110 us (level)
  blocking collectives: 96 us -> 93.6 us
    all_to_all x5, blocking collectives: 96 us -> 93.6 us  [exchange(): return lax.all_to_all(value, axes, 0, 0, tiled=True)]
where the time goes in v6:
time: 110 us; the launch traced here: 109 us
  blocking collectives  93.6 us (85%)
  Pallas kernels  7.88 us (7%)
  waiting for transfers between devices  4.61 us (4%)
  starting transfers between devices  2.09 us (2%)
    all_to_all x5, blocking collectives, exchange(): return lax.all_to_all(value, axes, 0, 0, tiled=True)  93.6 us
    ppermute x1, waiting for transfers between devices, body(): raw_next = lax.ppermute(raw, LAG + PAR, down)  4.61 us
    pallas_call x1, Pallas kernels, body(): pl.pallas_call(tile_zero_kernel, out_shape=sent, grid=(STEPS,), in_specs=...  4.41 us
    pallas_call x5, Pallas kernels, call(): pl.pallas_call(kernel, out_shape=out_shape, in_specs=[VMEM] * len(args),...  3.48 us
  transfers between devices with their start and end apart: 2, of which 1 were waited for; matrix products, arithmetic and copies ran while one was open for 0% of the time, Pallas kernels for 4%

profile of v6, /device:TPU:2, one launch (start us, length us, event | category | flops | bytes accessed | tf_op | source)
XLA Modules:
  0.0 109.4 jit_solution(16959230269656687035)
XLA Ops:
  0.6 0.8 collective-permute-start.1
  1.4 1.3 %collective-permute-start = (bf16[512,2048]{1,0:T(8,128)(2,1)}, bf16[512,2048]{1,0:T(8,128)(2,1)S(1)}, u32[]{:S(2)}, u32[]{:S(2)}) collective-permute-start(bf16[512,2048]{1,0:T(8,128)(2,1)} %bitcast.11), channel_id=1, source_target_pairs={{8,0},{10,2},{12,4},{14,6},{16,8},{18,10},{20,12},{22,14},{24,16},... | collective-permute-start | bytes 6291464 | tf_op jit(solution)/shard_map/ppermute | solution.py:193
  2.7 4.4 %shard_map.41 = f32[4,2,8,4224]{3,2,1,0:T(8,128)S(1)} custom-call(bf16[512,2048]{1,0:T(8,128)(2,1)} %bitcast.9, bf16[512,2048]{1,0:T(8,128)(2,1)} %bitcast.12), custom_call_target="tpu_custom_call" | custom-call | tf_op jit(solution)/shard_map/pallas_call | solution.py:198
  7.1 0.0 copy-start
  7.2 0.0 copy-start.1
  7.2 0.1 convert_element_type.26
  7.2 17.6 %all_to_all.25 = f16[8,8,4224]{2,1,0:T(8,128)(2,1)S(1)} all-to-all(f16[8,8,4224]{2,1,0:T(8,128)(2,1)S(1)} %bitcast.14), channel_id=1, replica_groups=mesh['zh'=4,'zl'=4,'y'=4,'x'=4,'core'=2] {'x','core'}, dimensions={0} | all-to-all | bytes 1081344 | tf_op jit(solution)/shard_map/all_to_all | solution.py:177
  24.9 0.1 convert.2.zero
  24.9 0.0 collective-permute-done.1.prior_last
  25.0 4.6 %collective-permute-done.raw_next = bf16[512,2048]{1,0:T(8,128)(2,1)S(1)} collective-permute-done((bf16[512,2048]{1,0:T(8,128)(2,1)}, bf16[512,2048]{1,0:T(8,128)(2,1)S(1)}, u32[]{:S(2)}, u32[]{:S(2)}) %collective-permute-start) | collective-permute-done | bytes 2097184 | tf_op jit(solution)/shard_map/ppermute | solution.py:193
  29.6 0.0 copy-done
  29.6 0.0 copy-done.1
  29.6 1.5 %shard_map.42 = f32[4,2,8,4224]{3,2,1,0:T(8,128)S(1)} custom-call(bf16[512,2048]{1,0:T(8,128)(2,1)S(1)} %bitcast.10, bf16[512,2048]{1,0:T(8,128)(2,1)S(1)} %collective-permute-done.raw_next, bf16[512,2048]{1,0:T(8,128)(2,1)S(1)} %collective-permute-done.1.prior_last, bf16[512,2048]{1,0:T(8,128)(2,1)S(1)} %bitcast.13), custom_call_target="tpu_custom_call" | custom-call | tf_op jit(solution)/shard_map/pallas_call | solution.py:27
  31.0 0.1 convert_element_type.28
  31.1 17.4 %all_to_all.26 = f16[8,8,4224]{2,1,0:T(8,128)(2,1)S(1)} all-to-all(f16[8,8,4224]{2,1,0:T(8,128)(2,1)S(1)} %bitcast.16), channel_id=1, replica_groups=mesh['zh'=4,'zl'=4,'y'=4,'x'=4,'core'=2] {'x','core'}, dimensions={0} | all-to-all | bytes 1081344 | tf_op jit(solution)/shard_map/all_to_all | solution.py:177
  48.5 0.1 convert.3.one
  48.5 0.5 shard_map.43
  49.1 19.3 %all_to_all.27 = f16[16,72,128]{2,1,0:T(8,128)(2,1)S(1)} all-to-all(f16[16,72,128]{2,1,0:T(8,128)(2,1)S(1)} %convert_element_type.30), channel_id=1, replica_groups=mesh['zh'=4,'zl'=4,'y'=4,'x'=4,'core'=2] {'zl','y'}, dimensions={0} | all-to-all | bytes 589824 | tf_op jit(solution)/shard_map/all_to_all | solution.py:177
  68.5 0.3 shard_map.44
  68.8 25.9 %all_to_all.28.total = f32[4,48,128]{2,1,0:T(8,128)S(1)} all-to-all(f32[4,48,128]{2,1,0:T(8,128)S(1)} %get-tuple-element.11), channel_id=1, replica_groups=mesh['zh'=4,'zl'=4,'y'=4,'x'=4,'core'=2] {'zh'}, dimensions={0} | all-to-all | bytes 196608 | tf_op jit(solution)/shard_map/all_to_all | solution.py:177
  94.7 0.3 shard_map.45
  95.0 13.5 %all_to_all.29 = f16[16,48,128]{2,1,0:T(8,128)(2,1)S(1)} all-to-all(f16[16,48,128]{2,1,0:T(8,128)(2,1)S(1)} %convert_element_type.32), channel_id=1, replica_groups=mesh['zh'=4,'zl'=4,'y'=4,'x'=4,'core'=2] {'zl','y'}, dimensions={0} | all-to-all | bytes 393216 | tf_op jit(solution)/shard_map/all_to_all | solution.py:177
  108.5 0.9 shard_map.46
  (4 shorter events, 0.1 us)
Async XLA Ops:
  0.6 24.3 %collective-permute-start.1 = (bf16[512,2048]{1,0:T(8,128)(2,1)}, bf16[512,2048]{1,0:T(8,128)(2,1)S(1)}, u32[]{:S(2)}, u32[]{:S(2)}) collective-permute-start(bf16[512,2048]{1,0:T(8,128)(2,1)} %bitcast.8), channel_id=1, source_target_pairs={{1,9},{3,11},{5,13},{7,15},{9,17},{11,19},{13,21},{15,23},{17,25},... | collective-permute-start | bytes 6291464 | tf_op jit(solution)/shard_map/ppermute | solution.py:194
  1.4 28.1 %collective-permute-start = (bf16[512,2048]{1,0:T(8,128)(2,1)}, bf16[512,2048]{1,0:T(8,128)(2,1)S(1)}, u32[]{:S(2)}, u32[]{:S(2)}) collective-permute-start(bf16[512,2048]{1,0:T(8,128)(2,1)} %bitcast.11), channel_id=1, source_target_pairs={{8,0},{10,2},{12,4},{14,6},{16,8},{18,10},{20,12},{22,14},{24,16},... | collective-permute-start | bytes 6291464 | tf_op jit(solution)/shard_map/ppermute | solution.py:193
  7.1 22.4 %copy-start = (bf16[1,512,2048]{2,1,0:T(8,128)(2,1)S(1)}, bf16[1,512,2048]{2,1,0:T(8,128)(2,1)}, u32[]{:S(2)}) copy-start(bf16[1,512,2048]{2,1,0:T(8,128)(2,1)} %param.2) | copy-start | bytes 6291460
  7.2 22.4 %copy-start.1 = (bf16[1,512,2048]{2,1,0:T(8,128)(2,1)S(1)}, bf16[1,512,2048]{2,1,0:T(8,128)(2,1)}, u32[]{:S(2)}) copy-start(bf16[1,512,2048]{2,1,0:T(8,128)(2,1)} %param.3) | copy-start | bytes 6291460

commit v7 on v6

v7 whole, which is shorter than its diff:
```python
import jax
import jax.numpy as jnp
import numpy as np
from jax import lax
from jax.experimental import pallas as pl
from jax.experimental.pallas import tpu as pltpu
from jax.sharding import Mesh, PartitionSpec as P

F32 = jnp.float32
F16 = jnp.float16
NT = (((1,), (1,)), ((), ()))
LAG = ("zh", "zl", "y")
PAR = ("x", "core")
VMEM = pl.BlockSpec(memory_space=pltpu.VMEM)


def near(value):
    return pltpu.with_memory_space_constraint(value, pltpu.VMEM)


def call(kernel, out_shape, *args):
    return pl.pallas_call(
        kernel,
        out_shape=out_shape,
        in_specs=[VMEM] * len(args),
        out_specs=jax.tree.map(lambda _: VMEM, out_shape),
        compiler_params=pltpu.CompilerParams(vmem_limit_bytes=6 * 2**20),
    )(*[near(arg) for arg in args])


def shape(*dims):
    return pltpu.VMEM(dims, F32)


def result(*dims):
    return jax.ShapeDtypeStruct(dims, F32)


def exponent_of(value):
    top = jnp.max(jnp.max(jnp.abs(value), axis=0, keepdims=True), axis=1, keepdims=True)
    return jnp.floor(jnp.log2(jnp.maximum(top, 1e-30)))


LEVEL = 3.3


def encode(value, exponent):
    size = jnp.abs(value) * jnp.exp2(7.0 - exponent)
    binade = jnp.floor(jnp.log2(jnp.maximum(size, 1.0)))
    place = LEVEL * (binade + size * jnp.exp2(-binade))
    whole = jnp.floor(place)
    code = jnp.exp2(whole - 14.0) * (1.0 + (place - whole))
    return jnp.where(value < 0, -code, code)


def decode(code, exponent):
    size = jnp.abs(code)
    whole = jnp.floor(jnp.log2(jnp.maximum(size, 2.0**-14)))
    place = (whole + 13.0 + size * jnp.exp2(-whole)) * (1.0 / LEVEL)
    binade = jnp.maximum(jnp.floor(place) - 1.0, 0.0)
    value = (place - binade) * jnp.exp2(binade + exponent - 7.0)
    return jnp.where(code < 0, -value, value)


def pack(tile, height, out):
    exponent = exponent_of(tile)
    tail = jnp.broadcast_to(exponent, (8, 128))
    sent = tile * jnp.exp2(14.0 - exponent)
    for owner in range(8):
        groups = [sent[first : first + 8] for first in range(owner * height, (owner + 1) * height, 8)]
        out[owner] = jnp.concatenate(groups + [tail], axis=1)


def summed(parts, width):
    lanes = parts[0].shape[1] - 128
    groups = [None] * (lanes // width)
    for part in parts:
        scale = jnp.exp2(part[:, lanes:] - 14.0)
        scale = jnp.concatenate([scale] * (width // 128), axis=1)
        for i in range(len(groups)):
            group = part[:, i * width : (i + 1) * width] * scale
            groups[i] = group if groups[i] is None else groups[i] + group
    return jnp.concatenate(groups, axis=0)


def picked(prior, raw, half, out, sems):
    def copies(source, first, step):
        rows = [(source.at[pl.ds(first + i * step, 32)], out.at[pl.ds(i * 32, 32)]) for i in range(8)]
        return [pltpu.make_async_copy(here, there, sems.at[i]) for i, (here, there) in enumerate(rows)]

    return copies(raw, half * 256, 32), copies(prior, half * 32, 64)


def run(copies):
    for copy in copies:
        copy.start()
    for copy in copies:
        copy.wait()


def first_half_kernel(prior, raw, out, sems):
    from_raw, from_prior = picked(prior, raw, 0, out, sems)
    core = lax.axis_index("core")
    pl.when(core == 0)(lambda: run(from_raw))
    pl.when(core == 1)(lambda: run(from_prior))


def second_half_kernel(prior, raw, out, prior_near, raw_near, sems):
    from_raw, from_prior = picked(prior, raw, 1, out, sems)
    whole = []
    for i in range(4):
        rows = pl.ds(i * 128, 128)
        whole.append(pltpu.make_async_copy(prior.at[rows], prior_near.at[rows], sems.at[8 + i]))
        whole.append(pltpu.make_async_copy(raw.at[rows], raw_near.at[rows], sems.at[12 + i]))
    core = lax.axis_index("core")
    pl.when(core == 0)(lambda: run(from_raw + whole))
    pl.when(core == 1)(lambda: run(from_prior + whole))


def fetch(kernel, out_shape, copies, prior, raw):
    far = [pltpu.with_memory_space_constraint(value, pltpu.HBM) for value in (prior, raw)]
    return pl.pallas_call(
        kernel,
        out_shape=out_shape,
        in_specs=[pl.BlockSpec(memory_space=pltpu.HBM)] * 2,
        out_specs=jax.tree.map(lambda _: VMEM, out_shape),
        scratch_shapes=[pltpu.SemaphoreType.DMA((copies,))],
        compiler_params=pltpu.CompilerParams(vmem_limit_bytes=2 * 2**20),
    )(*far)


def tile_zero_kernel(prior, raw, out):
    pack(lax.dot_general(prior[...], raw[...], NT, preferred_element_type=F32), 64, out)


def tile_one_kernel(prior, raw, moved, out):
    def form(left, right, height):
        pack(lax.dot_general(left[...], right[...], NT, preferred_element_type=F32), height, out)

    core = lax.axis_index("core")
    pl.when(core == 0)(lambda: form(prior, moved, 64))
    pl.when(core == 1)(lambda: form(moved, raw, 32))


def spread_kernel(zero, one_a, one_b, out):
    whole = summed([zero[i] for i in range(8)], 512)
    here = jnp.concatenate([summed([one[i] for i in range(0, 8, 2)], 256) for one in (one_a, one_b)], axis=1)
    late = jnp.concatenate([summed([one[i] for i in range(1, 8, 2)], 512) for one in (one_a, one_b)], axis=0)
    for i, value in enumerate((whole, here, late)):
        exponent = exponent_of(value)
        value = encode(value, exponent)
        for zl in range(4):
            for y in range(4):
                out[zl * 4 + y, i * 16 : (i + 1) * 16] = value[y * 16 : (y + 1) * 16, zl * 128 : (zl + 1) * 128]
                out[zl * 4 + y, 48 + i * 8 : 56 + i * 8] = jnp.broadcast_to(exponent, (8, 128))


def block_prefix_kernel(lags, local, total):
    def read(lag, i):
        exponent = lags[lag, 48 + i * 8 : 56 + i * 8]
        exponent = jnp.concatenate([exponent, exponent], axis=0)
        return decode(lags[lag, i * 16 : (i + 1) * 16], exponent)

    zero, one = jnp.zeros((16, 128), F32), jnp.zeros((16, 128), F32)
    lates = [read(lag, 2) for lag in range(16)]
    for lag in range(16):
        zero = zero + read(lag, 0)
        one = one + read(lag, 1) + lates[lag]
        local[lag, 0:16] = zero
        local[lag, 16:32] = one + lates[lag + 1] if lag < 15 else one
    for i in range(4):
        total[i, 0:16] = zero
        total[i, 16:32] = one
        total[i, 32:48] = lates[0]


def finish_kernel(local, total, out):
    place = lax.axis_index("zh")
    earlier, late = jnp.zeros((32, 128), F32), jnp.zeros((16, 128), F32)
    for z in range(4):
        earlier = earlier + jnp.where(z < place, total[z, 0:32], 0.0)
        late = late + jnp.where(z == place + 1, total[z, 32:48], 0.0)
    for i in range(16):
        out[i] = local[i] + earlier
    out[15, 16:32] = local[15, 16:32] + earlier[16:32] + late


def split_kernel(rows, zero, one):
    for zl in range(4):
        for y in range(4):
            here, there = slice(y * 16, (y + 1) * 16), slice(zl * 128, (zl + 1) * 128)
            zero[0, here, there] = rows[zl * 4 + y, 0:16]
            one[0, here, there] = rows[zl * 4 + y, 16:32]


def exchange(value, axes):
    return lax.all_to_all(value, axes, 0, 0, tiled=True)


def exchange_short(value, axes):
    return exchange(value.astype(F16), axes).astype(F32)


def body(prior_rows, raw_rows):
    prior, raw = prior_rows[0], raw_rows[0]
    device = np.arange(512).reshape(64, 4, 2)
    down = [(int(device[l + 1, x, 0]), int(device[l, x, 0])) for l in range(63) for x in range(4)]
    up = [(int(device[l, x, 1]), int(device[l + 1, x, 1])) for l in range(63) for x in range(4)]

    half = pltpu.VMEM((256, 2048), jnp.bfloat16)
    full = pltpu.VMEM((512, 2048), jnp.bfloat16)
    sent = fetch(first_half_kernel, half, 8, prior, raw)
    moved_a = lax.ppermute(sent, LAG + PAR, down + up)
    sent, prior, raw = fetch(second_half_kernel, (half, full, full), 16, prior, raw)
    moved_b = lax.ppermute(sent, LAG + PAR, down + up)

    zero = exchange_short(call(tile_zero_kernel, shape(8, 8, 4224), prior, raw), PAR)
    moved_a, zero = lax.optimization_barrier((moved_a, zero))
    one_a = exchange_short(call(tile_one_kernel, shape(8, 8, 2176), prior, raw, moved_a), PAR)
    moved_b, one_a = lax.optimization_barrier((moved_b, one_a))
    one_b = exchange_short(call(tile_one_kernel, shape(8, 8, 2176), prior, raw, moved_b), PAR)

    lags = exchange_short(call(spread_kernel, shape(16, 72, 128), zero, one_a, one_b), ("zl", "y"))
    local, total = call(block_prefix_kernel, (shape(16, 32, 128), shape(4, 48, 128)), lags)
    rows = call(finish_kernel, shape(16, 32, 128), local, exchange(total, "zh"))
    return tuple(call(split_kernel, (result(1, 64, 512), result(1, 64, 512)), exchange(rows, ("zl", "y"))))


def solution(mesh):
    chips = Mesh(mesh.devices.reshape(4, 4, 4, 4, 2), LAG + PAR)
    in_specs = (P(LAG, None, PAR), P(LAG, None, PAR))
    out_specs = (P(LAG, PAR, None), P(LAG, PAR, None))
    return jax.shard_map(body, mesh=chips, in_specs=in_specs, out_specs=out_specs, check_vma=False)
```

time: 110 us -> 110 us (level)
  waiting for transfers between devices: 4.61 us -> 0.01 us
  blocking collectives: 93.6 us -> 97.1 us
    ppermute x2, waiting for transfers between devices: 4.61 us -> 0.01 us  [the longest x1 0.01 us: body(): moved_b = lax.ppermute(sent, LAG + PAR, down + up)]
    all_to_all x5 -> x6, blocking collectives: 93.6 us -> 97.1 us  [exchange(): return lax.all_to_all(value, axes, 0, 0, tiled=True)]
    pallas_call x5 -> x7, Pallas kernels: 3.48 us -> 4.81 us  [call(): pl.pallas_call(kernel, out_shape=out_shape, in_specs=[VMEM] * len(args),...]
    pallas_call x1 -> x2, Pallas kernels: 4.41 us -> 4.08 us  [fetch(): pl.pallas_call(kernel, out_shape=out_shape, in_specs=[pl.BlockSpec(memory...]
  transfers between devices with their start and end apart: 2 -> 2, of which waited for: 1 -> 0; matrix products, arithmetic and copies ran while one was open for 0% -> 0% of each run, Pallas kernels for 4% -> 5%
where the time goes in v7:
time: 110 us
  blocking collectives  97.1 us (88%)
  Pallas kernels  8.88 us (8%)
  starting transfers between devices  2.58 us (2%)
    all_to_all x6, blocking collectives, exchange(): return lax.all_to_all(value, axes, 0, 0, tiled=True)  97.1 us
    pallas_call x7, Pallas kernels, call(): pl.pallas_call(kernel, out_shape=out_shape, in_specs=[VMEM] * len(args),...  4.81 us
    pallas_call x2, Pallas kernels, fetch(): pl.pallas_call(kernel, out_shape=out_shape, in_specs=[pl.BlockSpec(memory...  4.08 us
  transfers between devices with their start and end apart: 2, of which 0 were waited for; matrix products, arithmetic and copies ran while one was open for 0% of the time, Pallas kernels for 5%

profile of v7, /device:TPU:2, one launch (start us, length us, event | category | flops | bytes accessed | tf_op | source)
XLA Modules:
  0.0 109.7 jit_solution(12319032666741319482)
XLA Ops:
  0.6 1.4 %shard_map.41 = bf16[256,2048]{1,0:T(8,128)(2,1)S(1)} custom-call(bf16[512,2048]{1,0:T(8,128)(2,1)} %bitcast.2, bf16[512,2048]{1,0:T(8,128)(2,1)} %bitcast.4), custom_call_target="tpu_custom_call" | custom-call | tf_op jit(solution)/shard_map/pallas_call | solution.py:122
  2.0 1.3 %collective-permute-start = (bf16[256,2048]{1,0:T(8,128)(2,1)S(1)}, bf16[256,2048]{1,0:T(8,128)(2,1)S(1)}, u32[]{:S(2)}, u32[]{:S(2)}) collective-permute-start(bf16[256,2048]{1,0:T(8,128)(2,1)S(1)} %shard_map.41), channel_id=1, source_target_pairs={{8,0},{10,2},{12,4},{14,6},{16,8},{18,10},{20,12},{22,14},{24,16},... | collective-permute-start | bytes 3145736 | tf_op jit(solution)/shard_map/ppermute | solution.py:213
  3.3 2.7 %shard_map.42 = (bf16[256,2048]{1,0:T(8,128)(2,1)S(1)}, bf16[512,2048]{1,0:T(8,128)(2,1)S(1)}, bf16[512,2048]{1,0:T(8,128)(2,1)S(1)}) custom-call(bf16[512,2048]{1,0:T(8,128)(2,1)} %bitcast.3, bf16[512,2048]{1,0:T(8,128)(2,1)} %bitcast.5), custom_call_target="tpu_custom_call" | custom-call | tf_op jit(solution)/shard_map/pallas_call | solution.py:122
  6.0 1.3 %collective-permute-start.1 = (bf16[256,2048]{1,0:T(8,128)(2,1)S(1)}, bf16[256,2048]{1,0:T(8,128)(2,1)S(1)}, u32[]{:S(2)}, u32[]{:S(2)}) collective-permute-start(bf16[256,2048]{1,0:T(8,128)(2,1)S(1)} %get-tuple-element.14), channel_id=1, source_target_pairs={{8,0},{10,2},{12,4},{14,6},{16,8},{18,10},{20,12},{22,14},{24,16},... | collective-permute-start | bytes 3145736 | tf_op jit(solution)/shard_map/ppermute | solution.py:215
  7.3 1.4 %shard_map.43 = f32[8,8,4224]{2,1,0:T(8,128)S(1)} custom-call(bf16[512,2048]{1,0:T(8,128)(2,1)S(1)} %get-tuple-element.11.prior, bf16[512,2048]{1,0:T(8,128)(2,1)S(1)} %get-tuple-element.12.raw), custom_call_target="tpu_custom_call" | custom-call | tf_op jit(solution)/shard_map/pallas_call | solution.py:22
  8.8 0.1 convert_element_type.24
  8.8 17.4 %all_to_all.30 = f16[8,8,4224]{2,1,0:T(8,128)(2,1)S(1)} all-to-all(f16[8,8,4224]{2,1,0:T(8,128)(2,1)S(1)} %convert_element_type.24), channel_id=1, replica_groups=mesh['zh'=4,'zl'=4,'y'=4,'x'=4,'core'=2] {'x','core'}, dimensions={0} | all-to-all | bytes 1081344 | tf_op jit(solution)/shard_map/all_to_all | solution.py:197
  26.2 0.1 convert_element_type.25.zero
  26.3 0.0 collective-permute-done.moved
  26.3 0.9 shard_map.44
  27.2 10.1 %all_to_all.31 = f16[8,8,2176]{2,1,0:T(8,128)(2,1)S(1)} all-to-all(f16[8,8,2176]{2,1,0:T(8,128)(2,1)S(1)} %convert_element_type.26), channel_id=1, replica_groups=mesh['zh'=4,'zl'=4,'y'=4,'x'=4,'core'=2] {'x','core'}, dimensions={0} | all-to-all | bytes 557056 | tf_op jit(solution)/shard_map/all_to_all | solution.py:197
  37.4 0.0 collective-permute-done.1.moved
  37.4 0.9 shard_map.45
  38.3 10.1 %all_to_all.32 = f16[8,8,2176]{2,1,0:T(8,128)(2,1)S(1)} all-to-all(f16[8,8,2176]{2,1,0:T(8,128)(2,1)S(1)} %convert_element_type.28), channel_id=1, replica_groups=mesh['zh'=4,'zl'=4,'y'=4,'x'=4,'core'=2] {'x','core'}, dimensions={0} | all-to-all | bytes 557056 | tf_op jit(solution)/shard_map/all_to_all | solution.py:197
  48.4 0.5 shard_map.46
  49.0 20.5 %all_to_all.33 = f16[16,72,128]{2,1,0:T(8,128)(2,1)S(1)} all-to-all(f16[16,72,128]{2,1,0:T(8,128)(2,1)S(1)} %convert_element_type.30), channel_id=1, replica_groups=mesh['zh'=4,'zl'=4,'y'=4,'x'=4,'core'=2] {'zl','y'}, dimensions={0} | all-to-all | bytes 589824 | tf_op jit(solution)/shard_map/all_to_all | solution.py:197
  69.6 0.3 shard_map.47
  69.9 25.1 %all_to_all.34.total = f32[4,48,128]{2,1,0:T(8,128)S(1)} all-to-all(f32[4,48,128]{2,1,0:T(8,128)S(1)} %get-tuple-element.19), channel_id=1, replica_groups=mesh['zh'=4,'zl'=4,'y'=4,'x'=4,'core'=2] {'zh'}, dimensions={0} | all-to-all | bytes 196608 | tf_op jit(solution)/shard_map/all_to_all | solution.py:197
  95.0 14.0 %all_to_all.35.rows = f32[16,32,128]{2,1,0:T(8,128)S(1)} all-to-all(f32[16,32,128]{2,1,0:T(8,128)S(1)} %shard_map.48), channel_id=1, replica_groups=mesh['zh'=4,'zl'=4,'y'=4,'x'=4,'core'=2] {'zl','y'}, dimensions={0} | all-to-all | bytes 524288 | tf_op jit(solution)/shard_map/all_to_all | solution.py:197
  109.0 0.7 shard_map.49
  (7 shorter events, 0.2 us)
Async XLA Ops:
  2.0 24.3 %collective-permute-start = (bf16[256,2048]{1,0:T(8,128)(2,1)S(1)}, bf16[256,2048]{1,0:T(8,128)(2,1)S(1)}, u32[]{:S(2)}, u32[]{:S(2)}) collective-permute-start(bf16[256,2048]{1,0:T(8,128)(2,1)S(1)} %shard_map.41), channel_id=1, source_target_pairs={{8,0},{10,2},{12,4},{14,6},{16,8},{18,10},{20,12},{22,14},{24,16},... | collective-permute-start | bytes 3145736 | tf_op jit(solution)/shard_map/ppermute | solution.py:213
  6.0 31.4 %collective-permute-start.1 = (bf16[256,2048]{1,0:T(8,128)(2,1)S(1)}, bf16[256,2048]{1,0:T(8,128)(2,1)S(1)}, u32[]{:S(2)}, u32[]{:S(2)}) collective-permute-start(bf16[256,2048]{1,0:T(8,128)(2,1)S(1)} %get-tuple-element.14), channel_id=1, source_target_pairs={{8,0},{10,2},{12,4},{14,6},{16,8},{18,10},{20,12},{22,14},{24,16},... | collective-permute-start | bytes 3145736 | tf_op jit(solution)/shard_map/ppermute | solution.py:215

commit v8 on v5

--- a/solution.py
+++ b/solution.py
@@ -46,7 +46,28 @@
     return jnp.floor(jnp.log2(jnp.maximum(top, 1e-30)))
 
 
-def pack(tile, out):
+LEVEL = 3.3
+
+
+def encode(value, exponent):
+    size = jnp.abs(value) * jnp.exp2(7.0 - exponent)
+    binade = jnp.floor(jnp.log2(jnp.maximum(size, 1.0)))
+    place = LEVEL * (binade + size * jnp.exp2(-binade))
+    whole = jnp.floor(place)
+    code = jnp.exp2(whole - 14.0) * (1.0 + (place - whole))
+    return jnp.where(value < 0, -code, code)
+
+
+def decode(code, exponent):
+    size = jnp.abs(code)
+    whole = jnp.floor(jnp.log2(jnp.maximum(size, 2.0**-14)))
+    place = (whole + 13.0 + size * jnp.exp2(-whole)) * (1.0 / LEVEL)
+    binade = jnp.maximum(jnp.floor(place) - 1.0, 0.0)
+    value = (place - binade) * jnp.exp2(binade + exponent - 7.0)
+    return jnp.where(code < 0, -value, value)
+
+
+def pack_rows(tile, out):
     exponent = exponent_of(tile)
     tail = jnp.broadcast_to(exponent, (8, 128))
     sent = tile * jnp.exp2(14.0 - exponent)
@@ -57,7 +78,7 @@
             out[x, c] = jnp.concatenate(groups + [tail], axis=1)
 
 
-def summed(parts):
+def summed_rows(parts):
     groups = [None] * 8
     for part in parts:
         scale = jnp.exp2(part[:, 4096:] - 14.0)
@@ -68,6 +89,32 @@
     return jnp.concatenate(groups, axis=0)
 
 
+def pack_blocks(tile, out):
+    exponent = exponent_of(tile)
+    tail = jnp.broadcast_to(exponent, (8, 128))
+    sent = tile * jnp.exp2(14.0 - exponent)
+    for x in range(4):
+        for c in range(2):
+            for y in range(4):
+                first = x * 128 + c * 64 + y * 16
+                top, bottom = sent[first : first + 8], sent[first + 8 : first + 16]
+                out[y, x, c] = jnp.concatenate([top, bottom, tail], axis=1)
+
+
+def unpack(sent):
+    scale = jnp.exp2(sent[:, 1024:] - 14.0)
+    scale = jnp.concatenate([scale] * 4, axis=1)
+    return sent[:, :512] * scale, sent[:, 512:1024] * scale
+
+
+def summed_blocks(parts):
+    top, bottom = unpack(parts[0])
+    for part in parts[1:]:
+        more_top, more_bottom = unpack(part)
+        top, bottom = top + more_top, bottom + more_bottom
+    return jnp.concatenate([top, bottom], axis=0)
+
+
 def tile_zero_kernel(prior, raw, out, total):
     step = pl.program_id(0)
     part = lax.dot_general(prior[...], raw[...], NT, preferred_element_type=F32)
@@ -82,38 +129,64 @@
 
     @pl.when(step == STEPS - 1)
     def _():
-        pack(total[...], out)
+        pack_rows(total[...], out)
 
 
 def tile_one_kernel(prior, raw_next, prior_last, raw, out):
     def form(left, right):
-        pack(lax.dot_general(left[...], right[...], NT, preferred_element_type=F32), out)
+        pack_blocks(lax.dot_general(left[...], right[...], NT, preferred_element_type=F32), out)
 
     core = lax.axis_index("core")
     pl.when(core == 0)(lambda: form(prior, raw_next))
     pl.when(core == 1)(lambda: form(prior_last, raw))
 
 
-def spread_kernel(zero, one, out):
-    whole = summed([zero[x, c] for x in range(4) for c in range(2)])
-    here, late = (summed([one[x, c] for x in range(4)]) for c in range(2))
-    for i, value in enumerate((whole, here, late)):
+def add_kernel(parts, out):
+    out[...] = summed_rows([parts[x, c] for x in range(4) for c in range(2)])
+
+
+def plane_prefix_kernel(zero, one, out):
+    zeros, ones, late = [], [], None
+    for lag in range(4):
+        zeros.append(zero[lag] if lag == 0 else zeros[-1] + zero[lag])
+        here, after = (summed_blocks([one[lag, x, c] for x in range(4)]) for c in range(2))
+        if lag == 0:
+            late, total = after, here + after
+        else:
+            ones.append(total + after)
+            total = total + here + after
+    ones.append(total)
+    first = 0
+    for i, parts in enumerate((zeros, ones, [late])):
+        value = jnp.concatenate(parts, axis=0)
+        exponent = exponent_of(value)
+        value = encode(value, exponent)
+        height = value.shape[0]
         for zl in range(4):
-            for y in range(4):
-                out[zl * 4 + y, i * 16 : (i + 1) * 16] = value[y * 16 : (y + 1) * 16, zl * 128 : (zl + 1) * 128]
-
-
-def block_prefix_kernel(lags, local, total):
+            out[zl, first : first + height] = value[:, zl * 128 : (zl + 1) * 128]
+            out[zl, 144 + i * 8 : 152 + i * 8] = jnp.broadcast_to(exponent, (8, 128))
+        first += height
+
+
+def block_prefix_kernel(planes, local, total):
+    def read(zl, i, first):
+        exponent = planes[zl, 144 + i * 8 : 152 + i * 8]
+        exponent = jnp.concatenate([exponent, exponent], axis=0)
+        return decode(planes[zl, first : first + 16], exponent)
+
     zero, one = jnp.zeros((16, 128), F32), jnp.zeros((16, 128), F32)
-    for lag in range(16):
-        zero = zero + lags[lag, 0:16]
-        one = one + lags[lag, 16:32] + lags[lag, 32:48]
-        local[lag, 0:16] = zero
-        local[lag, 16:32] = one + lags[lag + 1, 32:48] if lag < 15 else one
+    lates = [read(zl, 2, 128) for zl in range(4)]
+    for zl in range(4):
+        for lag in range(4):
+            here_zero = zero + read(zl, 0, lag * 16)
+            here_one = one + read(zl, 1, 64 + lag * 16)
+            local[zl * 4 + lag, 0:16] = here_zero
+            local[zl * 4 + lag, 16:32] = here_one + lates[zl + 1] if lag == 3 and zl < 3 else here_one
+        zero, one = here_zero, here_one
     for i in range(4):
         total[i, 0:16] = zero
         total[i, 16:32] = one
-        total[i, 32:48] = lags[0, 32:48]
+        total[i, 32:48] = lates[0]
 
 
 def finish_kernel(local, total, out):
@@ -139,9 +212,8 @@
     return lax.all_to_all(value, axes, 0, 0, tiled=True)
 
 
-def reduce_rows(tile):
-    tile = exchange(tile.reshape(8, 8, 4224).astype(F16), PAR)
-    return tile.astype(F32).reshape(4, 2, 8, 4224)
+def exchange_short(value, axes):
+    return exchange(value.astype(F16), axes).astype(F32)
 
 
 def body(prior_rows, raw_rows):
@@ -152,24 +224,25 @@
     raw_next = lax.ppermute(raw, LAG + PAR, down)
     prior_last = lax.ppermute(prior, LAG + PAR, up)
 
-    sent = shape(4, 2, 8, 4224)
     piece = pl.BlockSpec((512, 2048 // STEPS), lambda step: (0, step))
     zero = pl.pallas_call(
         tile_zero_kernel,
-        out_shape=sent,
+        out_shape=shape(4, 2, 8, 4224),
         grid=(STEPS,),
         in_specs=[piece, piece],
         out_specs=VMEM,
         scratch_shapes=[pltpu.VMEM((512, 512), F32)],
         compiler_params=pltpu.CompilerParams(vmem_limit_bytes=8 * 2**20),
     )(far(prior), far(raw))
-    zero = reduce_rows(zero)
+    zero = exchange_short(zero.reshape(8, 8, 4224), PAR).reshape(4, 2, 8, 4224)
+    zero = exchange(call(add_kernel, shape(64, 512), zero).reshape(4, 16, 512), "y")
 
     raw_next, prior_last, zero = lax.optimization_barrier((raw_next, prior_last, zero))
-    one = reduce_rows(call(tile_one_kernel, sent, prior, raw_next, prior_last, raw))
-
-    lags = exchange(call(spread_kernel, shape(16, 48, 128), zero, one), ("zl", "y"))
-    local, total = call(block_prefix_kernel, (shape(16, 32, 128), shape(4, 48, 128)), lags)
+    one = call(tile_one_kernel, shape(4, 4, 2, 8, 1152), prior, raw_next, prior_last, raw)
+    one = exchange_short(one.reshape(32, 8, 1152), ("y", "x", "core")).reshape(4, 4, 2, 8, 1152)
+
+    planes = exchange_short(call(plane_prefix_kernel, shape(4, 168, 128), zero, one), "zl")
+    local, total = call(block_prefix_kernel, (shape(16, 32, 128), shape(4, 48, 128)), planes)
     rows = call(finish_kernel, shape(16, 32, 128), local, exchange(total, "zh"))
     return tuple(call(split_kernel, (result(1, 64, 512), result(1, 64, 512)), exchange(rows, ("zl", "y"))))
 

time: 111 us -> 109 us (0.982)
  waiting for transfers between devices: 4.61 us -> 0.01 us
  blocking collectives: 96 us -> 98.5 us
    ppermute x1, waiting for transfers between devices: 4.61 us -> 0.01 us  [body(): raw_next = lax.ppermute(raw, LAG + PAR, down)]
    all_to_all x5 -> x6, blocking collectives: 96 us -> 98.5 us  [exchange(): return lax.all_to_all(value, axes, 0, 0, tiled=True)]
    pallas_call x5 -> x6, Pallas kernels: 2.39 us -> 2.87 us  [call(): pl.pallas_call(kernel, out_shape=out_shape, in_specs=[VMEM] * len(args),...]
  transfers between devices with their start and end apart: 2 -> 2, of which waited for: 1 -> 0; matrix products, arithmetic and copies ran while one was open for 0% -> 0% of each run, Pallas kernels for 4% -> 4%
where the time goes in v8:
time: 109 us
  blocking collectives  98.5 us (90%)
  Pallas kernels  7.28 us (7%)
  starting transfers between devices  2.09 us (2%)
    all_to_all x6, blocking collectives, exchange(): return lax.all_to_all(value, axes, 0, 0, tiled=True)  98.5 us
    pallas_call x1, Pallas kernels, body(): pl.pallas_call(tile_zero_kernel, out_shape=shape(4, 2, 8, 4224), grid=(ST...  4.41 us
    pallas_call x6, Pallas kernels, call(): pl.pallas_call(kernel, out_shape=out_shape, in_specs=[VMEM] * len(args),...  2.87 us
  transfers between devices with their start and end apart: 2, of which 0 were waited for; matrix products, arithmetic and copies ran while one was open for 0% of the time, Pallas kernels for 4%

profile of v8, /device:TPU:2, one launch (start us, length us, event | category | flops | bytes accessed | tf_op | source)
XLA Modules:
  0.0 109.0 jit_solution(9253819447856835293)
XLA Ops:
  0.6 0.8 collective-permute-start.1
  1.4 1.3 %collective-permute-start = (bf16[512,2048]{1,0:T(8,128)(2,1)}, bf16[512,2048]{1,0:T(8,128)(2,1)S(1)}, u32[]{:S(2)}, u32[]{:S(2)}) collective-permute-start(bf16[512,2048]{1,0:T(8,128)(2,1)} %bitcast.12), channel_id=1, source_target_pairs={{8,0},{10,2},{12,4},{14,6},{16,8},{18,10},{20,12},{22,14},{24,16},... | collective-permute-start | bytes 6291464 | tf_op jit(solution)/shard_map/ppermute | solution.py:224
  2.7 4.4 %shard_map.41 = f32[4,2,8,4224]{3,2,1,0:T(8,128)S(1)} custom-call(bf16[512,2048]{1,0:T(8,128)(2,1)} %bitcast.10, bf16[512,2048]{1,0:T(8,128)(2,1)} %bitcast.13), custom_call_target="tpu_custom_call" | custom-call | tf_op jit(solution)/shard_map/pallas_call | solution.py:228
  7.1 0.0 copy-start.1
  7.2 0.1 convert_element_type.20
  7.2 0.0 copy-start
  7.2 17.6 %all_to_all.30 = f16[8,8,4224]{2,1,0:T(8,128)(2,1)S(1)} all-to-all(f16[8,8,4224]{2,1,0:T(8,128)(2,1)S(1)} %bitcast.18), channel_id=1, replica_groups=mesh['zh'=4,'zl'=4,'y'=4,'x'=4,'core'=2] {'x','core'}, dimensions={0} | all-to-all | bytes 1081344 | tf_op jit(solution)/shard_map/all_to_all | solution.py:212
  24.9 0.1 convert.2.parts
  24.9 0.1 shard_map.42
  25.0 9.7 %all_to_all.31.zero = f32[4,16,512]{2,1,0:T(8,128)S(1)} all-to-all(f32[4,16,512]{2,1,0:T(8,128)S(1)} %bitcast.15), channel_id=1, replica_groups=mesh['zh'=4,'zl'=4,'y'=4,'x'=4,'core'=2] {'y'}, dimensions={0} | all-to-all | bytes 262144 | tf_op jit(solution)/shard_map/all_to_all | solution.py:212
  34.7 0.0 collective-permute-done.1.prior_last
  34.7 0.0 collective-permute-done.raw_next
  34.7 0.0 copy-done.1
  34.7 0.0 copy-done
  34.7 1.5 %shard_map.43 = f32[4,4,2,8,1152]{4,3,2,1,0:T(8,128)S(1)} custom-call(bf16[512,2048]{1,0:T(8,128)(2,1)S(1)} %bitcast.11, bf16[512,2048]{1,0:T(8,128)(2,1)S(1)} %collective-permute-done.raw_next, bf16[512,2048]{1,0:T(8,128)(2,1)S(1)} %collective-permute-done.1.prior_last, bf16[512,2048]{1,0:T(8,128)(2,1)S(1)} %bitcast.14), custom_call_target="tpu_custom_call" | custom-call | tf_op jit(solution)/shard_map/pallas_call | solution.py:27
  36.2 0.1 convert_element_type.22
  36.3 17.1 %all_to_all.32 = f16[32,8,1152]{2,1,0:T(8,128)(2,1)S(1)} all-to-all(f16[32,8,1152]{2,1,0:T(8,128)(2,1)S(1)} %bitcast.16), channel_id=1, replica_groups=mesh['zh'=4,'zl'=4,'y'=4,'x'=4,'core'=2] {'y','x','core'}, dimensions={0} | all-to-all | bytes 1179648 | tf_op jit(solution)/shard_map/all_to_all | solution.py:212
  53.4 0.1 convert.3.one
  53.5 0.4 shard_map.44
  53.9 14.0 %all_to_all.33 = f16[4,168,128]{2,1,0:T(8,128)(2,1)S(1)} all-to-all(f16[4,168,128]{2,1,0:T(8,128)(2,1)S(1)} %convert_element_type.24), channel_id=1, replica_groups=mesh['zh'=4,'zl'=4,'y'=4,'x'=4,'core'=2] {'zl'}, dimensions={0} | all-to-all | bytes 344064 | tf_op jit(solution)/shard_map/all_to_all | solution.py:212
  67.9 0.2 shard_map.45
  68.2 25.6 %all_to_all.34.total = f32[4,48,128]{2,1,0:T(8,128)S(1)} all-to-all(f32[4,48,128]{2,1,0:T(8,128)S(1)} %get-tuple-element.11), channel_id=1, replica_groups=mesh['zh'=4,'zl'=4,'y'=4,'x'=4,'core'=2] {'zh'}, dimensions={0} | all-to-all | bytes 196608 | tf_op jit(solution)/shard_map/all_to_all | solution.py:212
  93.8 14.5 %all_to_all.35.rows = f32[16,32,128]{2,1,0:T(8,128)S(1)} all-to-all(f32[16,32,128]{2,1,0:T(8,128)S(1)} %shard_map.46), channel_id=1, replica_groups=mesh['zh'=4,'zl'=4,'y'=4,'x'=4,'core'=2] {'zl','y'}, dimensions={0} | all-to-all | bytes 524288 | tf_op jit(solution)/shard_map/all_to_all | solution.py:212
  108.3 0.7 shard_map.47
  (3 shorter events, 0.1 us)
Async XLA Ops:
  0.6 34.1 %collective-permute-start.1 = (bf16[512,2048]{1,0:T(8,128)(2,1)}, bf16[512,2048]{1,0:T(8,128)(2,1)S(1)}, u32[]{:S(2)}, u32[]{:S(2)}) collective-permute-start(bf16[512,2048]{1,0:T(8,128)(2,1)} %bitcast.9), channel_id=1, source_target_pairs={{1,9},{3,11},{5,13},{7,15},{9,17},{11,19},{13,21},{15,23},{17,25},... | collective-permute-start | bytes 6291464 | tf_op jit(solution)/shard_map/ppermute | solution.py:225
  1.4 33.3 %collective-permute-start = (bf16[512,2048]{1,0:T(8,128)(2,1)}, bf16[512,2048]{1,0:T(8,128)(2,1)S(1)}, u32[]{:S(2)}, u32[]{:S(2)}) collective-permute-start(bf16[512,2048]{1,0:T(8,128)(2,1)} %bitcast.12), channel_id=1, source_target_pairs={{8,0},{10,2},{12,4},{14,6},{16,8},{18,10},{20,12},{22,14},{24,16},... | collective-permute-start | bytes 6291464 | tf_op jit(solution)/shard_map/ppermute | solution.py:224
  7.1 27.6 %copy-start.1 = (bf16[1,512,2048]{2,1,0:T(8,128)(2,1)S(1)}, bf16[1,512,2048]{2,1,0:T(8,128)(2,1)}, u32[]{:S(2)}) copy-start(bf16[1,512,2048]{2,1,0:T(8,128)(2,1)} %param.3) | copy-start | bytes 6291460
  7.2 27.5 %copy-start = (bf16[1,512,2048]{2,1,0:T(8,128)(2,1)S(1)}, bf16[1,512,2048]{2,1,0:T(8,128)(2,1)}, u32[]{:S(2)}) copy-start(bf16[1,512,2048]{2,1,0:T(8,128)(2,1)} %param.2) | copy-start | bytes 6291460

commit v9 on v8

--- a/solution.py
+++ b/solution.py
@@ -5,6 +5,7 @@
 from jax.experimental import pallas as pl
 from jax.experimental.pallas import tpu as pltpu
 from jax.sharding import Mesh, PartitionSpec as P
+
 
 F32 = jnp.float32
 F16 = jnp.float16
@@ -168,7 +169,7 @@
         first += height
 
 
-def block_prefix_kernel(planes, local, total):
+def block_prefix_kernel(planes, local, total, late):
     def read(zl, i, first):
         exponent = planes[zl, 144 + i * 8 : 152 + i * 8]
         exponent = jnp.concatenate([exponent, exponent], axis=0)
@@ -183,21 +184,19 @@
             local[zl * 4 + lag, 0:16] = here_zero
             local[zl * 4 + lag, 16:32] = here_one + lates[zl + 1] if lag == 3 and zl < 3 else here_one
         zero, one = here_zero, here_one
-    for i in range(4):
-        total[i, 0:16] = zero
-        total[i, 16:32] = one
-        total[i, 32:48] = lates[0]
-
-
-def finish_kernel(local, total, out):
-    place = lax.axis_index("zh")
-    earlier, late = jnp.zeros((32, 128), F32), jnp.zeros((16, 128), F32)
-    for z in range(4):
-        earlier = earlier + jnp.where(z < place, total[z, 0:32], 0.0)
-        late = late + jnp.where(z == place + 1, total[z, 32:48], 0.0)
+    total[0:16], total[16:32] = zero, one
+    late[...] = lates[0]
+
+
+def sum_kernel(left, right, out):
+    out[...] = left[...] + right[...]
+
+
+def finish_kernel(local, first, second, third, late, out):
+    earlier = first[...] + second[...] + third[...]
     for i in range(16):
         out[i] = local[i] + earlier
-    out[15, 16:32] = local[15, 16:32] + earlier[16:32] + late
+    out[15, 16:32] = local[15, 16:32] + earlier[16:32] + late[...]
 
 
 def split_kernel(rows, zero, one):
@@ -242,8 +241,15 @@
     one = exchange_short(one.reshape(32, 8, 1152), ("y", "x", "core")).reshape(4, 4, 2, 8, 1152)
 
     planes = exchange_short(call(plane_prefix_kernel, shape(4, 168, 128), zero, one), "zl")
-    local, total = call(block_prefix_kernel, (shape(16, 32, 128), shape(4, 48, 128)), planes)
-    rows = call(finish_kernel, shape(16, 32, 128), local, exchange(total, "zh"))
+    shapes = shape(16, 32, 128), shape(32, 128), shape(16, 128)
+    local, total, late = call(block_prefix_kernel, shapes, planes)
+    late = lax.ppermute(late, "zh", [(1, 0), (2, 1), (3, 2)])
+    first = lax.ppermute(total, "zh", [(0, 1)])
+    total = call(sum_kernel, shape(32, 128), total, first)
+    second = lax.ppermute(total, "zh", [(1, 2)])
+    total = call(sum_kernel, shape(32, 128), total, second)
+    third = lax.ppermute(total, "zh", [(2, 3)])
+    rows = call(finish_kernel, shape(16, 32, 128), local, first, second, third, late)
     return tuple(call(split_kernel, (result(1, 64, 512), result(1, 64, 512)), exchange(rows, ("zl", "y"))))
 
 

time: 109 us -> 107 us (0.982)
  the two profiles are of different devices: /device:TPU:2 before, /device:TPU:128 now
where the time goes in v9:
time: 107 us
  blocking collectives  69.7 us (65%)
  waiting for transfers between devices  18.1 us (17%)
  starting transfers between devices  10.4 us (10%)
  Pallas kernels  7.29 us (7%)
    all_to_all x5, blocking collectives, exchange(): return lax.all_to_all(value, axes, 0, 0, tiled=True)  69.7 us
    ppermute x1, waiting for transfers between devices, body(): late = lax.ppermute(late, 'zh', [(1, 0), (2, 1), (3, 2)])  8.44 us
    ppermute x1, waiting for transfers between devices, body(): first = lax.ppermute(total, 'zh', [(0, 1)])  8.24 us
    ppermute x1, starting transfers between devices, body(): raw_next = lax.ppermute(raw, LAG + PAR, down)  4.47 us
    pallas_call x1, Pallas kernels, body(): pl.pallas_call(tile_zero_kernel, out_shape=shape(4, 2, 8, 4224), grid=(ST...  4.41 us
    pallas_call x8, Pallas kernels, call(): pl.pallas_call(kernel, out_shape=out_shape, in_specs=[VMEM] * len(args),...  2.88 us
  transfers between devices with their start and end apart: 6, of which 3 were waited for; matrix products, arithmetic and copies ran while one was open for 0% of the time, Pallas kernels for 4%

profile of v9, /device:TPU:128, one launch (start us, length us, event | category | flops | bytes accessed | tf_op | source)
XLA Modules:
  0.0 106.7 jit_solution(12737439712751755437)
XLA Ops:
  0.6 0.8 collective-permute-start.1
  1.4 4.5 %collective-permute-start = (bf16[512,2048]{1,0:T(8,128)(2,1)}, bf16[512,2048]{1,0:T(8,128)(2,1)S(1)}, u32[]{:S(2)}, u32[]{:S(2)}) collective-permute-start(bf16[512,2048]{1,0:T(8,128)(2,1)} %bitcast.12), channel_id=1, source_target_pairs={{8,0},{10,2},{12,4},{14,6},{16,8},{18,10},{20,12},{22,14},{24,16},... | collective-permute-start | bytes 6291464 | tf_op jit(solution)/shard_map/ppermute | solution.py:223
  5.9 4.4 %shard_map.41 = f32[4,2,8,4224]{3,2,1,0:T(8,128)S(1)} custom-call(bf16[512,2048]{1,0:T(8,128)(2,1)} %bitcast.10, bf16[512,2048]{1,0:T(8,128)(2,1)} %bitcast.13), custom_call_target="tpu_custom_call" | custom-call | tf_op jit(solution)/shard_map/pallas_call | solution.py:227
  10.3 0.0 copy-start.1
  10.3 0.1 convert_element_type.20
  10.4 0.0 copy-start
  10.4 14.9 %all_to_all.25 = f16[8,8,4224]{2,1,0:T(8,128)(2,1)S(1)} all-to-all(f16[8,8,4224]{2,1,0:T(8,128)(2,1)S(1)} %bitcast.18), channel_id=1, replica_groups=mesh['zh'=4,'zl'=4,'y'=4,'x'=4,'core'=2] {'x','core'}, dimensions={0} | all-to-all | bytes 1081344 | tf_op jit(solution)/shard_map/all_to_all | solution.py:211
  25.3 0.1 convert.2.parts
  25.4 0.1 shard_map.42
  25.5 8.4 %all_to_all.26.zero = f32[4,16,512]{2,1,0:T(8,128)S(1)} all-to-all(f32[4,16,512]{2,1,0:T(8,128)S(1)} %bitcast.15), channel_id=1, replica_groups=mesh['zh'=4,'zl'=4,'y'=4,'x'=4,'core'=2] {'y'}, dimensions={0} | all-to-all | bytes 262144 | tf_op jit(solution)/shard_map/all_to_all | solution.py:211
  33.8 0.0 collective-permute-done.1.prior_last
  33.8 0.0 collective-permute-done.raw_next
  33.8 0.0 copy-done.1
  33.8 0.0 copy-done
  33.9 1.5 %shard_map.43 = f32[4,4,2,8,1152]{4,3,2,1,0:T(8,128)S(1)} custom-call(bf16[512,2048]{1,0:T(8,128)(2,1)S(1)} %bitcast.11, bf16[512,2048]{1,0:T(8,128)(2,1)S(1)} %collective-permute-done.raw_next, bf16[512,2048]{1,0:T(8,128)(2,1)S(1)} %collective-permute-done.1.prior_last, bf16[512,2048]{1,0:T(8,128)(2,1)S(1)} %bitcast.14), custom_call_target="tpu_custom_call" | custom-call | tf_op jit(solution)/shard_map/pallas_call | solution.py:28
  35.3 0.1 convert_element_type.22
  35.4 18.5 %all_to_all.27 = f16[32,8,1152]{2,1,0:T(8,128)(2,1)S(1)} all-to-all(f16[32,8,1152]{2,1,0:T(8,128)(2,1)S(1)} %bitcast.16), channel_id=1, replica_groups=mesh['zh'=4,'zl'=4,'y'=4,'x'=4,'core'=2] {'y','x','core'}, dimensions={0} | all-to-all | bytes 1179648 | tf_op jit(solution)/shard_map/all_to_all | solution.py:211
  53.9 0.1 convert.3.one
  54.0 0.4 shard_map.44
  54.4 14.1 %all_to_all.28 = f16[4,168,128]{2,1,0:T(8,128)(2,1)S(1)} all-to-all(f16[4,168,128]{2,1,0:T(8,128)(2,1)S(1)} %convert_element_type.24), channel_id=1, replica_groups=mesh['zh'=4,'zl'=4,'y'=4,'x'=4,'core'=2] {'zl'}, dimensions={0} | all-to-all | bytes 344064 | tf_op jit(solution)/shard_map/all_to_all | solution.py:211
  68.5 0.2 shard_map.45
  68.8 1.3 %collective-permute-start.2 = (f32[32,128]{1,0:T(8,128)S(1)}, f32[32,128]{1,0:T(8,128)S(1)}, u32[]{:S(2)}, u32[]{:S(2)}) collective-permute-start(f32[32,128]{1,0:T(8,128)S(1)} %get-tuple-element.12.left), channel_id=1, source_target_pairs={{0,128},{1,129},{2,130},{3,131},{4,132},{5,133},{6,134},{7,135},{8... | collective-permute-start | bytes 49160 | tf_op jit(solution)/shard_map/ppermute | solution.py:247
  70.1 8.2 %collective-permute-done.2.right.first = f32[32,128]{1,0:T(8,128)S(1)} collective-permute-done((f32[32,128]{1,0:T(8,128)S(1)}, f32[32,128]{1,0:T(8,128)S(1)}, u32[]{:S(2)}, u32[]{:S(2)}) %collective-permute-start.2) | collective-permute-done | bytes 16416 | tf_op jit(solution)/shard_map/ppermute | solution.py:247
  78.3 1.3 %collective-permute-start.3 = (f32[32,128]{1,0:T(8,128)S(1)}, f32[32,128]{1,0:T(8,128)S(1)}, u32[]{:S(2)}, u32[]{:S(2)}) collective-permute-start(f32[32,128]{1,0:T(8,128)S(1)} %shard_map.46.left), channel_id=1, source_target_pairs={{128,256},{129,257},{130,258},{131,259},{132,260},{133,261},{134,2... | collective-permute-start | bytes 49160 | tf_op jit(solution)/shard_map/ppermute | solution.py:249
  79.6 1.4 %collective-permute-done.3.right.second = f32[32,128]{1,0:T(8,128)S(1)} collective-permute-done((f32[32,128]{1,0:T(8,128)S(1)}, f32[32,128]{1,0:T(8,128)S(1)}, u32[]{:S(2)}, u32[]{:S(2)}) %collective-permute-start.3) | collective-permute-done | bytes 16416 | tf_op jit(solution)/shard_map/ppermute | solution.py:249
  81.0 0.7 collective-permute-start.4
  81.7 1.9 %collective-permute-start.5 = (f32[16,128]{1,0:T(8,128)S(1)}, f32[16,128]{1,0:T(8,128)S(1)}, u32[]{:S(2)}, u32[]{:S(2)}) collective-permute-start(f32[16,128]{1,0:T(8,128)S(1)} %get-tuple-element.13), channel_id=1, source_target_pairs={{128,0},{256,128},{384,256},{129,1},{257,129},{385,257},{130,2},{2... | collective-permute-start | bytes 24584 | tf_op jit(solution)/shard_map/ppermute | solution.py:246
  83.6 8.4 %collective-permute-done.5.late = f32[16,128]{1,0:T(8,128)S(1)} collective-permute-done((f32[16,128]{1,0:T(8,128)S(1)}, f32[16,128]{1,0:T(8,128)S(1)}, u32[]{:S(2)}, u32[]{:S(2)}) %collective-permute-start.5) | collective-permute-done | bytes 8224 | tf_op jit(solution)/shard_map/ppermute | solution.py:246
  92.1 0.0 collective-permute-done.4.third
  92.1 13.9 %all_to_all.29.rows = f32[16,32,128]{2,1,0:T(8,128)S(1)} all-to-all(f32[16,32,128]{2,1,0:T(8,128)S(1)} %shard_map.48), channel_id=1, replica_groups=mesh['zh'=4,'zl'=4,'y'=4,'x'=4,'core'=2] {'zl','y'}, dimensions={0} | all-to-all | bytes 524288 | tf_op jit(solution)/shard_map/all_to_all | solution.py:211
  106.0 0.7 shard_map.49
  (5 shorter events, 0.1 us)
Async XLA Ops:
  0.6 33.2 %collective-permute-start.1 = (bf16[512,2048]{1,0:T(8,128)(2,1)}, bf16[512,2048]{1,0:T(8,128)(2,1)S(1)}, u32[]{:S(2)}, u32[]{:S(2)}) collective-permute-start(bf16[512,2048]{1,0:T(8,128)(2,1)} %bitcast.9), channel_id=1, source_target_pairs={{1,9},{3,11},{5,13},{7,15},{9,17},{11,19},{13,21},{15,23},{17,25},... | collective-permute-start | bytes 6291464 | tf_op jit(solution)/shard_map/ppermute | solution.py:224
  1.4 32.4 %collective-permute-start = (bf16[512,2048]{1,0:T(8,128)(2,1)}, bf16[512,2048]{1,0:T(8,128)(2,1)S(1)}, u32[]{:S(2)}, u32[]{:S(2)}) collective-permute-start(bf16[512,2048]{1,0:T(8,128)(2,1)} %bitcast.12), channel_id=1, source_target_pairs={{8,0},{10,2},{12,4},{14,6},{16,8},{18,10},{20,12},{22,14},{24,16},... | collective-permute-start | bytes 6291464 | tf_op jit(solution)/shard_map/ppermute | solution.py:223
  10.3 23.5 %copy-start.1 = (bf16[1,512,2048]{2,1,0:T(8,128)(2,1)S(1)}, bf16[1,512,2048]{2,1,0:T(8,128)(2,1)}, u32[]{:S(2)}) copy-start(bf16[1,512,2048]{2,1,0:T(8,128)(2,1)} %param.3) | copy-start | bytes 6291460
  10.4 23.4 %copy-start = (bf16[1,512,2048]{2,1,0:T(8,128)(2,1)S(1)}, bf16[1,512,2048]{2,1,0:T(8,128)(2,1)}, u32[]{:S(2)}) copy-start(bf16[1,512,2048]{2,1,0:T(8,128)(2,1)} %param.2) | copy-start | bytes 6291460
  68.8 9.5 %collective-permute-start.2 = (f32[32,128]{1,0:T(8,128)S(1)}, f32[32,128]{1,0:T(8,128)S(1)}, u32[]{:S(2)}, u32[]{:S(2)}) collective-permute-start(f32[32,128]{1,0:T(8,128)S(1)} %get-tuple-element.12.left), channel_id=1, source_target_pairs={{0,128},{1,129},{2,130},{3,131},{4,132},{5,133},{6,134},{7,135},{8... | collective-permute-start | bytes 49160 | tf_op jit(solution)/shard_map/ppermute | solution.py:247
  78.3 2.7 %collective-permute-start.3 = (f32[32,128]{1,0:T(8,128)S(1)}, f32[32,128]{1,0:T(8,128)S(1)}, u32[]{:S(2)}, u32[]{:S(2)}) collective-permute-start(f32[32,128]{1,0:T(8,128)S(1)} %shard_map.46.left), channel_id=1, source_target_pairs={{128,256},{129,257},{130,258},{131,259},{132,260},{133,261},{134,2... | collective-permute-start | bytes 49160 | tf_op jit(solution)/shard_map/ppermute | solution.py:249
  81.0 11.0 %collective-permute-start.4 = (f32[32,128]{1,0:T(8,128)S(1)}, f32[32,128]{1,0:T(8,128)S(1)}, u32[]{:S(2)}, u32[]{:S(2)}) collective-permute-start(f32[32,128]{1,0:T(8,128)S(1)} %shard_map.47), channel_id=1, source_target_pairs={{256,384},{257,385},{258,386},{259,387},{260,388},{261,389},{262,3... | collective-permute-start | bytes 49160 | tf_op jit(solution)/shard_map/ppermute | solution.py:251
  81.7 10.4 %collective-permute-start.5 = (f32[16,128]{1,0:T(8,128)S(1)}, f32[16,128]{1,0:T(8,128)S(1)}, u32[]{:S(2)}, u32[]{:S(2)}) collective-permute-start(f32[16,128]{1,0:T(8,128)S(1)} %get-tuple-element.13), channel_id=1, source_target_pairs={{128,0},{256,128},{384,256},{129,1},{257,129},{385,257},{130,2},{2... | collective-permute-start | bytes 24584 | tf_op jit(solution)/shard_map/ppermute | solution.py:246

commit v10 on v8

--- a/solution.py
+++ b/solution.py
@@ -5,6 +5,7 @@
 from jax.experimental import pallas as pl
 from jax.experimental.pallas import tpu as pltpu
 from jax.sharding import Mesh, PartitionSpec as P
+
 
 F32 = jnp.float32
 F16 = jnp.float16
@@ -183,18 +184,22 @@
             local[zl * 4 + lag, 0:16] = here_zero
             local[zl * 4 + lag, 16:32] = here_one + lates[zl + 1] if lag == 3 and zl < 3 else here_one
         zero, one = here_zero, here_one
-    for i in range(4):
-        total[i, 0:16] = zero
-        total[i, 16:32] = one
-        total[i, 32:48] = lates[0]
-
-
-def finish_kernel(local, total, out):
+    total[0:16], total[16:32], total[32:48] = zero, one, lates[0]
+
+
+def sum_kernel(total, other, out):
+    out[0:32] = total[0:32] + other[0:32]
+    out[32:48] = total[32:48]
+
+
+def finish_kernel(local, early, crossed, own, out):
     place = lax.axis_index("zh")
-    earlier, late = jnp.zeros((32, 128), F32), jnp.zeros((16, 128), F32)
-    for z in range(4):
-        earlier = earlier + jnp.where(z < place, total[z, 0:32], 0.0)
-        late = late + jnp.where(z == place + 1, total[z, 32:48], 0.0)
+
+    def pick(chosen, ref, first, last):
+        return jnp.where(chosen, ref[first:last], 0.0)
+
+    earlier = pick(place == 1, early, 0, 32) + pick(place >= 2, crossed, 0, 32) + pick(place == 3, own, 0, 32)
+    late = pick(place == 0, early, 32, 48) + pick(place == 1, crossed, 32, 48) + pick(place == 2, own, 32, 48)
     for i in range(16):
         out[i] = local[i] + earlier
     out[15, 16:32] = local[15, 16:32] + earlier[16:32] + late
@@ -242,8 +247,12 @@
     one = exchange_short(one.reshape(32, 8, 1152), ("y", "x", "core")).reshape(4, 4, 2, 8, 1152)
 
     planes = exchange_short(call(plane_prefix_kernel, shape(4, 168, 128), zero, one), "zl")
-    local, total = call(block_prefix_kernel, (shape(16, 32, 128), shape(4, 48, 128)), planes)
-    rows = call(finish_kernel, shape(16, 32, 128), local, exchange(total, "zh"))
+    local, total = call(block_prefix_kernel, (shape(16, 32, 128), shape(48, 128)), planes)
+    early = lax.ppermute(total, "zh", [(0, 1), (1, 0)])
+    both = call(sum_kernel, shape(48, 128), total, early)
+    crossed = lax.ppermute(both, "zh", [(1, 2), (2, 1), (0, 3)])
+    own = lax.ppermute(total, "zh", [(2, 3), (3, 2)])
+    rows = call(finish_kernel, shape(16, 32, 128), local, early, crossed, own)
     return tuple(call(split_kernel, (result(1, 64, 512), result(1, 64, 512)), exchange(rows, ("zl", "y"))))
 
 

time: 109 us -> 103 us (0.945)
  the two profiles are of different devices: /device:TPU:2 before, /device:TPU:128 now
where the time goes in v10:
time: 103 us
  blocking collectives  69.5 us (67%)
  waiting for transfers between devices  15.1 us (15%)
  starting transfers between devices  9.76 us (9%)
  Pallas kernels  7.3 us (7%)
    all_to_all x5, blocking collectives, exchange(): return lax.all_to_all(value, axes, 0, 0, tiled=True)  69.5 us
    ppermute x1, waiting for transfers between devices, body(): crossed = lax.ppermute(both, 'zh', [(1, 2), (2, 1), (0, 3)])  8.1 us
    ppermute x1, waiting for transfers between devices, body(): early = lax.ppermute(total, 'zh', [(0, 1), (1, 0)])  7.03 us
    ppermute x1, starting transfers between devices, body(): raw_next = lax.ppermute(raw, LAG + PAR, down)  4.47 us
    pallas_call x1, Pallas kernels, body(): pl.pallas_call(tile_zero_kernel, out_shape=shape(4, 2, 8, 4224), grid=(ST...  4.41 us
    pallas_call x7, Pallas kernels, call(): pl.pallas_call(kernel, out_shape=out_shape, in_specs=[VMEM] * len(args),...  2.88 us
  transfers between devices with their start and end apart: 5, of which 2 were waited for; matrix products, arithmetic and copies ran while one was open for 0% of the time, Pallas kernels for 4%

profile of v10, /device:TPU:128, one launch (start us, length us, event | category | flops | bytes accessed | tf_op | source)
XLA Modules:
  0.0 102.8 jit_solution(6057822286619746485)
XLA Ops:
  0.6 0.8 collective-permute-start.1
  1.4 4.5 %collective-permute-start = (bf16[512,2048]{1,0:T(8,128)(2,1)}, bf16[512,2048]{1,0:T(8,128)(2,1)S(1)}, u32[]{:S(2)}, u32[]{:S(2)}) collective-permute-start(bf16[512,2048]{1,0:T(8,128)(2,1)} %bitcast.12), channel_id=1, source_target_pairs={{8,0},{10,2},{12,4},{14,6},{16,8},{18,10},{20,12},{22,14},{24,16},... | collective-permute-start | bytes 6291464 | tf_op jit(solution)/shard_map/ppermute | solution.py:229
  5.9 4.4 %shard_map.41 = f32[4,2,8,4224]{3,2,1,0:T(8,128)S(1)} custom-call(bf16[512,2048]{1,0:T(8,128)(2,1)} %bitcast.10, bf16[512,2048]{1,0:T(8,128)(2,1)} %bitcast.13), custom_call_target="tpu_custom_call" | custom-call | tf_op jit(solution)/shard_map/pallas_call | solution.py:233
  10.3 0.0 copy-start.1
  10.3 0.1 convert_element_type.20
  10.4 0.0 copy-start
  10.4 14.9 %all_to_all.25 = f16[8,8,4224]{2,1,0:T(8,128)(2,1)S(1)} all-to-all(f16[8,8,4224]{2,1,0:T(8,128)(2,1)S(1)} %bitcast.18), channel_id=1, replica_groups=mesh['zh'=4,'zl'=4,'y'=4,'x'=4,'core'=2] {'x','core'}, dimensions={0} | all-to-all | bytes 1081344 | tf_op jit(solution)/shard_map/all_to_all | solution.py:217
  25.3 0.1 convert.2.parts
  25.4 0.1 shard_map.42
  25.5 8.4 %all_to_all.26.zero = f32[4,16,512]{2,1,0:T(8,128)S(1)} all-to-all(f32[4,16,512]{2,1,0:T(8,128)S(1)} %bitcast.15), channel_id=1, replica_groups=mesh['zh'=4,'zl'=4,'y'=4,'x'=4,'core'=2] {'y'}, dimensions={0} | all-to-all | bytes 262144 | tf_op jit(solution)/shard_map/all_to_all | solution.py:217
  33.8 0.0 collective-permute-done.1.prior_last
  33.8 0.0 collective-permute-done.raw_next
  33.8 0.0 copy-done.1
  33.8 0.0 copy-done
  33.9 1.5 %shard_map.43 = f32[4,4,2,8,1152]{4,3,2,1,0:T(8,128)S(1)} custom-call(bf16[512,2048]{1,0:T(8,128)(2,1)S(1)} %bitcast.11, bf16[512,2048]{1,0:T(8,128)(2,1)S(1)} %collective-permute-done.raw_next, bf16[512,2048]{1,0:T(8,128)(2,1)S(1)} %collective-permute-done.1.prior_last, bf16[512,2048]{1,0:T(8,128)(2,1)S(1)} %bitcast.14), custom_call_target="tpu_custom_call" | custom-call | tf_op jit(solution)/shard_map/pallas_call | solution.py:28
  35.3 0.1 convert_element_type.22
  35.4 18.5 %all_to_all.27 = f16[32,8,1152]{2,1,0:T(8,128)(2,1)S(1)} all-to-all(f16[32,8,1152]{2,1,0:T(8,128)(2,1)S(1)} %bitcast.16), channel_id=1, replica_groups=mesh['zh'=4,'zl'=4,'y'=4,'x'=4,'core'=2] {'y','x','core'}, dimensions={0} | all-to-all | bytes 1179648 | tf_op jit(solution)/shard_map/all_to_all | solution.py:217
  53.9 0.1 convert.3.one
  54.0 0.4 shard_map.44
  54.4 14.1 %all_to_all.28 = f16[4,168,128]{2,1,0:T(8,128)(2,1)S(1)} all-to-all(f16[4,168,128]{2,1,0:T(8,128)(2,1)S(1)} %convert_element_type.24), channel_id=1, replica_groups=mesh['zh'=4,'zl'=4,'y'=4,'x'=4,'core'=2] {'zl'}, dimensions={0} | all-to-all | bytes 344064 | tf_op jit(solution)/shard_map/all_to_all | solution.py:217
  68.5 0.2 shard_map.45
  68.8 1.9 %collective-permute-start.2 = (f32[48,128]{1,0:T(8,128)S(1)}, f32[48,128]{1,0:T(8,128)S(1)}, u32[]{:S(2)}, u32[]{:S(2)}) collective-permute-start(f32[48,128]{1,0:T(8,128)S(1)} %get-tuple-element.11.total), channel_id=1, source_target_pairs={{0,128},{128,0},{1,129},{129,1},{2,130},{130,2},{3,131},{131,3},{4... | collective-permute-start | bytes 73736 | tf_op jit(solution)/shard_map/ppermute | solution.py:251
  70.7 0.7 collective-permute-start.4
  71.4 7.0 %collective-permute-done.2.other.early = f32[48,128]{1,0:T(8,128)S(1)} collective-permute-done((f32[48,128]{1,0:T(8,128)S(1)}, f32[48,128]{1,0:T(8,128)S(1)}, u32[]{:S(2)}, u32[]{:S(2)}) %collective-permute-start.2) | collective-permute-done | bytes 24608 | tf_op jit(solution)/shard_map/ppermute | solution.py:251
  78.4 1.9 %collective-permute-start.3 = (f32[48,128]{1,0:T(8,128)S(1)}, f32[48,128]{1,0:T(8,128)S(1)}, u32[]{:S(2)}, u32[]{:S(2)}) collective-permute-start(f32[48,128]{1,0:T(8,128)S(1)} %shard_map.46), channel_id=1, source_target_pairs={{128,256},{256,128},{0,384},{129,257},{257,129},{1,385},{130,258},... | collective-permute-start | bytes 73736 | tf_op jit(solution)/shard_map/ppermute | solution.py:253
  80.3 0.0 collective-permute-done.4.own
  80.3 8.1 %collective-permute-done.3.crossed = f32[48,128]{1,0:T(8,128)S(1)} collective-permute-done((f32[48,128]{1,0:T(8,128)S(1)}, f32[48,128]{1,0:T(8,128)S(1)}, u32[]{:S(2)}, u32[]{:S(2)}) %collective-permute-start.3) | collective-permute-done | bytes 24608 | tf_op jit(solution)/shard_map/ppermute | solution.py:253
  88.5 13.6 %all_to_all.29.rows = f32[16,32,128]{2,1,0:T(8,128)S(1)} all-to-all(f32[16,32,128]{2,1,0:T(8,128)S(1)} %shard_map.47), channel_id=1, replica_groups=mesh['zh'=4,'zl'=4,'y'=4,'x'=4,'core'=2] {'zl','y'}, dimensions={0} | all-to-all | bytes 524288 | tf_op jit(solution)/shard_map/all_to_all | solution.py:217
  102.1 0.7 shard_map.48
  (4 shorter events, 0.1 us)
Async XLA Ops:
  0.6 33.2 %collective-permute-start.1 = (bf16[512,2048]{1,0:T(8,128)(2,1)}, bf16[512,2048]{1,0:T(8,128)(2,1)S(1)}, u32[]{:S(2)}, u32[]{:S(2)}) collective-permute-start(bf16[512,2048]{1,0:T(8,128)(2,1)} %bitcast.9), channel_id=1, source_target_pairs={{1,9},{3,11},{5,13},{7,15},{9,17},{11,19},{13,21},{15,23},{17,25},... | collective-permute-start | bytes 6291464 | tf_op jit(solution)/shard_map/ppermute | solution.py:230
  1.4 32.4 %collective-permute-start = (bf16[512,2048]{1,0:T(8,128)(2,1)}, bf16[512,2048]{1,0:T(8,128)(2,1)S(1)}, u32[]{:S(2)}, u32[]{:S(2)}) collective-permute-start(bf16[512,2048]{1,0:T(8,128)(2,1)} %bitcast.12), channel_id=1, source_target_pairs={{8,0},{10,2},{12,4},{14,6},{16,8},{18,10},{20,12},{22,14},{24,16},... | collective-permute-start | bytes 6291464 | tf_op jit(solution)/shard_map/ppermute | solution.py:229
  10.3 23.5 %copy-start.1 = (bf16[1,512,2048]{2,1,0:T(8,128)(2,1)S(1)}, bf16[1,512,2048]{2,1,0:T(8,128)(2,1)}, u32[]{:S(2)}) copy-start(bf16[1,512,2048]{2,1,0:T(8,128)(2,1)} %param.3) | copy-start | bytes 6291460
  10.4 23.4 %copy-start = (bf16[1,512,2048]{2,1,0:T(8,128)(2,1)S(1)}, bf16[1,512,2048]{2,1,0:T(8,128)(2,1)}, u32[]{:S(2)}) copy-start(bf16[1,512,2048]{2,1,0:T(8,128)(2,1)} %param.2) | copy-start | bytes 6291460
  68.8 9.6 %collective-permute-start.2 = (f32[48,128]{1,0:T(8,128)S(1)}, f32[48,128]{1,0:T(8,128)S(1)}, u32[]{:S(2)}, u32[]{:S(2)}) collective-permute-start(f32[48,128]{1,0:T(8,128)S(1)} %get-tuple-element.11.total), channel_id=1, source_target_pairs={{0,128},{128,0},{1,129},{129,1},{2,130},{130,2},{3,131},{131,3},{4... | collective-permute-start | bytes 73736 | tf_op jit(solution)/shard_map/ppermute | solution.py:251
  70.7 9.6 %collective-permute-start.4 = (f32[48,128]{1,0:T(8,128)S(1)}, f32[48,128]{1,0:T(8,128)S(1)}, u32[]{:S(2)}, u32[]{:S(2)}) collective-permute-start(f32[48,128]{1,0:T(8,128)S(1)} %get-tuple-element.11.total), channel_id=1, source_target_pairs={{256,384},{384,256},{257,385},{385,257},{258,386},{386,258},{259,3... | collective-permute-start | bytes 73736 | tf_op jit(solution)/shard_map/ppermute | solution.py:254
  78.4 10.0 %collective-permute-start.3 = (f32[48,128]{1,0:T(8,128)S(1)}, f32[48,128]{1,0:T(8,128)S(1)}, u32[]{:S(2)}, u32[]{:S(2)}) collective-permute-start(f32[48,128]{1,0:T(8,128)S(1)} %shard_map.46), channel_id=1, source_target_pairs={{128,256},{256,128},{0,384},{129,257},{257,129},{1,385},{130,258},... | collective-permute-start | bytes 73736 | tf_op jit(solution)/shard_map/ppermute | solution.py:253

commit v11 on v10

--- a/solution.py
+++ b/solution.py
@@ -192,14 +192,14 @@
     out[32:48] = total[32:48]
 
 
-def finish_kernel(local, early, crossed, own, out):
+def finish_kernel(local, early, back, crossed, own, out):
     place = lax.axis_index("zh")
 
     def pick(chosen, ref, first, last):
         return jnp.where(chosen, ref[first:last], 0.0)
 
     earlier = pick(place == 1, early, 0, 32) + pick(place >= 2, crossed, 0, 32) + pick(place == 3, own, 0, 32)
-    late = pick(place == 0, early, 32, 48) + pick(place == 1, crossed, 32, 48) + pick(place == 2, own, 32, 48)
+    late = pick(place == 0, early, 32, 48) + pick(place == 1, back, 32, 48) + pick(place == 2, own, 32, 48)
     for i in range(16):
         out[i] = local[i] + earlier
     out[15, 16:32] = local[15, 16:32] + earlier[16:32] + late
@@ -249,10 +249,11 @@
     planes = exchange_short(call(plane_prefix_kernel, shape(4, 168, 128), zero, one), "zl")
     local, total = call(block_prefix_kernel, (shape(16, 32, 128), shape(48, 128)), planes)
     early = lax.ppermute(total, "zh", [(0, 1), (1, 0)])
+    back = lax.ppermute(total, "zh", [(2, 1)])
     both = call(sum_kernel, shape(48, 128), total, early)
-    crossed = lax.ppermute(both, "zh", [(1, 2), (2, 1), (0, 3)])
+    crossed = lax.ppermute(both, "zh", [(1, 2), (0, 3)])
     own = lax.ppermute(total, "zh", [(2, 3), (3, 2)])
-    rows = call(finish_kernel, shape(16, 32, 128), local, early, crossed, own)
+    rows = call(finish_kernel, shape(16, 32, 128), local, early, back, crossed, own)
     return tuple(call(split_kernel, (result(1, 64, 512), result(1, 64, 512)), exchange(rows, ("zl", "y"))))
 
 

time: 103 us -> 101 us (0.981)
  the two profiles are of different devices: /device:TPU:128 before, /device:TPU:2 now
where the time goes in v11:
time: 101 us
  blocking collectives  71.7 us (71%)
  starting transfers between devices  17.5 us (17%)
  Pallas kernels  7.29 us (7%)
  waiting for transfers between devices  3.16 us (3%)
    all_to_all x5, blocking collectives, exchange(): return lax.all_to_all(value, axes, 0, 0, tiled=True)  71.7 us
    ppermute x1, starting transfers between devices, body(): early = lax.ppermute(total, 'zh', [(0, 1), (1, 0)])  9.1 us
    ppermute x1, starting transfers between devices, body(): crossed = lax.ppermute(both, 'zh', [(1, 2), (0, 3)])  5.02 us
    pallas_call x1, Pallas kernels, body(): pl.pallas_call(tile_zero_kernel, out_shape=shape(4, 2, 8, 4224), grid=(ST...  4.41 us
    pallas_call x7, Pallas kernels, call(): pl.pallas_call(kernel, out_shape=out_shape, in_specs=[VMEM] * len(args),...  2.88 us
  transfers between devices with their start and end apart: 6, of which 2 were waited for; matrix products, arithmetic and copies ran while one was open for 0% of the time, Pallas kernels for 4%

profile of v11, /device:TPU:2, one launch (start us, length us, event | category | flops | bytes accessed | tf_op | source)
XLA Modules:
  0.0 100.8 jit_solution(408559283374018052)
XLA Ops:
  0.6 0.8 collective-permute-start.1
  1.4 1.3 %collective-permute-start = (bf16[512,2048]{1,0:T(8,128)(2,1)}, bf16[512,2048]{1,0:T(8,128)(2,1)S(1)}, u32[]{:S(2)}, u32[]{:S(2)}) collective-permute-start(bf16[512,2048]{1,0:T(8,128)(2,1)} %bitcast.12), channel_id=1, source_target_pairs={{8,0},{10,2},{12,4},{14,6},{16,8},{18,10},{20,12},{22,14},{24,16},... | collective-permute-start | bytes 6291464 | tf_op jit(solution)/shard_map/ppermute | solution.py:229
  2.7 4.4 %shard_map.41 = f32[4,2,8,4224]{3,2,1,0:T(8,128)S(1)} custom-call(bf16[512,2048]{1,0:T(8,128)(2,1)} %bitcast.10, bf16[512,2048]{1,0:T(8,128)(2,1)} %bitcast.13), custom_call_target="tpu_custom_call" | custom-call | tf_op jit(solution)/shard_map/pallas_call | solution.py:233
  7.1 0.0 copy-start.1
  7.2 0.1 convert_element_type.20
  7.2 0.0 copy-start
  7.2 17.6 %all_to_all.25 = f16[8,8,4224]{2,1,0:T(8,128)(2,1)S(1)} all-to-all(f16[8,8,4224]{2,1,0:T(8,128)(2,1)S(1)} %bitcast.18), channel_id=1, replica_groups=mesh['zh'=4,'zl'=4,'y'=4,'x'=4,'core'=2] {'x','core'}, dimensions={0} | all-to-all | bytes 1081344 | tf_op jit(solution)/shard_map/all_to_all | solution.py:217
  24.9 0.1 convert.2.parts
  24.9 0.1 shard_map.42
  25.0 9.7 %all_to_all.26.zero = f32[4,16,512]{2,1,0:T(8,128)S(1)} all-to-all(f32[4,16,512]{2,1,0:T(8,128)S(1)} %bitcast.15), channel_id=1, replica_groups=mesh['zh'=4,'zl'=4,'y'=4,'x'=4,'core'=2] {'y'}, dimensions={0} | all-to-all | bytes 262144 | tf_op jit(solution)/shard_map/all_to_all | solution.py:217
  34.7 0.0 collective-permute-done.1.prior_last
  34.7 0.0 collective-permute-done.raw_next
  34.7 0.0 copy-done.1
  34.7 0.0 copy-done
  34.7 1.5 %shard_map.43 = f32[4,4,2,8,1152]{4,3,2,1,0:T(8,128)S(1)} custom-call(bf16[512,2048]{1,0:T(8,128)(2,1)S(1)} %bitcast.11, bf16[512,2048]{1,0:T(8,128)(2,1)S(1)} %collective-permute-done.raw_next, bf16[512,2048]{1,0:T(8,128)(2,1)S(1)} %collective-permute-done.1.prior_last, bf16[512,2048]{1,0:T(8,128)(2,1)S(1)} %bitcast.14), custom_call_target="tpu_custom_call" | custom-call | tf_op jit(solution)/shard_map/pallas_call | solution.py:28
  36.2 0.1 convert_element_type.22
  36.3 17.1 %all_to_all.27 = f16[32,8,1152]{2,1,0:T(8,128)(2,1)S(1)} all-to-all(f16[32,8,1152]{2,1,0:T(8,128)(2,1)S(1)} %bitcast.16), channel_id=1, replica_groups=mesh['zh'=4,'zl'=4,'y'=4,'x'=4,'core'=2] {'y','x','core'}, dimensions={0} | all-to-all | bytes 1179648 | tf_op jit(solution)/shard_map/all_to_all | solution.py:217
  53.4 0.1 convert.3.one
  53.5 0.4 shard_map.44
  53.9 14.0 %all_to_all.28 = f16[4,168,128]{2,1,0:T(8,128)(2,1)S(1)} all-to-all(f16[4,168,128]{2,1,0:T(8,128)(2,1)S(1)} %convert_element_type.24), channel_id=1, replica_groups=mesh['zh'=4,'zl'=4,'y'=4,'x'=4,'core'=2] {'zl'}, dimensions={0} | all-to-all | bytes 344064 | tf_op jit(solution)/shard_map/all_to_all | solution.py:217
  67.9 0.2 shard_map.45
  68.2 9.1 %collective-permute-start.2 = (f32[48,128]{1,0:T(8,128)S(1)}, f32[48,128]{1,0:T(8,128)S(1)}, u32[]{:S(2)}, u32[]{:S(2)}) collective-permute-start(f32[48,128]{1,0:T(8,128)S(1)} %get-tuple-element.11.total), channel_id=1, source_target_pairs={{0,128},{128,0},{1,129},{129,1},{2,130},{130,2},{3,131},{131,3},{4... | collective-permute-start | bytes 73736 | tf_op jit(solution)/shard_map/ppermute | solution.py:251
  77.3 0.7 collective-permute-start.5
  77.9 0.7 collective-permute-start.3
  78.6 1.4 %collective-permute-done.2.other.early = f32[48,128]{1,0:T(8,128)S(1)} collective-permute-done((f32[48,128]{1,0:T(8,128)S(1)}, f32[48,128]{1,0:T(8,128)S(1)}, u32[]{:S(2)}, u32[]{:S(2)}) %collective-permute-start.2) | collective-permute-done | bytes 24608 | tf_op jit(solution)/shard_map/ppermute | solution.py:251
  80.0 5.0 %collective-permute-start.4 = (f32[48,128]{1,0:T(8,128)S(1)}, f32[48,128]{1,0:T(8,128)S(1)}, u32[]{:S(2)}, u32[]{:S(2)}) collective-permute-start(f32[48,128]{1,0:T(8,128)S(1)} %shard_map.46), channel_id=1, source_target_pairs={{128,256},{0,384},{129,257},{1,385},{130,258},{2,386},{131,259},{3... | collective-permute-start | bytes 73736 | tf_op jit(solution)/shard_map/ppermute | solution.py:254
  85.0 0.0 collective-permute-done.5.own
  85.1 0.0 collective-permute-done.3.back
  85.1 1.8 %collective-permute-done.4.crossed = f32[48,128]{1,0:T(8,128)S(1)} collective-permute-done((f32[48,128]{1,0:T(8,128)S(1)}, f32[48,128]{1,0:T(8,128)S(1)}, u32[]{:S(2)}, u32[]{:S(2)}) %collective-permute-start.4) | collective-permute-done | bytes 24608 | tf_op jit(solution)/shard_map/ppermute | solution.py:254
  86.9 13.2 %all_to_all.29.rows = f32[16,32,128]{2,1,0:T(8,128)S(1)} all-to-all(f32[16,32,128]{2,1,0:T(8,128)S(1)} %shard_map.47), channel_id=1, replica_groups=mesh['zh'=4,'zl'=4,'y'=4,'x'=4,'core'=2] {'zl','y'}, dimensions={0} | all-to-all | bytes 524288 | tf_op jit(solution)/shard_map/all_to_all | solution.py:217
  100.1 0.7 shard_map.48
  (4 shorter events, 0.1 us)
Async XLA Ops:
  0.6 34.1 %collective-permute-start.1 = (bf16[512,2048]{1,0:T(8,128)(2,1)}, bf16[512,2048]{1,0:T(8,128)(2,1)S(1)}, u32[]{:S(2)}, u32[]{:S(2)}) collective-permute-start(bf16[512,2048]{1,0:T(8,128)(2,1)} %bitcast.9), channel_id=1, source_target_pairs={{1,9},{3,11},{5,13},{7,15},{9,17},{11,19},{13,21},{15,23},{17,25},... | collective-permute-start | bytes 6291464 | tf_op jit(solution)/shard_map/ppermute | solution.py:230
  1.4 33.3 %collective-permute-start = (bf16[512,2048]{1,0:T(8,128)(2,1)}, bf16[512,2048]{1,0:T(8,128)(2,1)S(1)}, u32[]{:S(2)}, u32[]{:S(2)}) collective-permute-start(bf16[512,2048]{1,0:T(8,128)(2,1)} %bitcast.12), channel_id=1, source_target_pairs={{8,0},{10,2},{12,4},{14,6},{16,8},{18,10},{20,12},{22,14},{24,16},... | collective-permute-start | bytes 6291464 | tf_op jit(solution)/shard_map/ppermute | solution.py:229
  7.1 27.6 %copy-start.1 = (bf16[1,512,2048]{2,1,0:T(8,128)(2,1)S(1)}, bf16[1,512,2048]{2,1,0:T(8,128)(2,1)}, u32[]{:S(2)}) copy-start(bf16[1,512,2048]{2,1,0:T(8,128)(2,1)} %param.3) | copy-start | bytes 6291460
  7.2 27.5 %copy-start = (bf16[1,512,2048]{2,1,0:T(8,128)(2,1)S(1)}, bf16[1,512,2048]{2,1,0:T(8,128)(2,1)}, u32[]{:S(2)}) copy-start(bf16[1,512,2048]{2,1,0:T(8,128)(2,1)} %param.2) | copy-start | bytes 6291460
  68.2 11.8 %collective-permute-start.2 = (f32[48,128]{1,0:T(8,128)S(1)}, f32[48,128]{1,0:T(8,128)S(1)}, u32[]{:S(2)}, u32[]{:S(2)}) collective-permute-start(f32[48,128]{1,0:T(8,128)S(1)} %get-tuple-element.11.total), channel_id=1, source_target_pairs={{0,128},{128,0},{1,129},{129,1},{2,130},{130,2},{3,131},{131,3},{4... | collective-permute-start | bytes 73736 | tf_op jit(solution)/shard_map/ppermute | solution.py:251
  77.3 7.8 %collective-permute-start.5 = (f32[48,128]{1,0:T(8,128)S(1)}, f32[48,128]{1,0:T(8,128)S(1)}, u32[]{:S(2)}, u32[]{:S(2)}) collective-permute-start(f32[48,128]{1,0:T(8,128)S(1)} %get-tuple-element.11.total), channel_id=1, source_target_pairs={{256,384},{384,256},{257,385},{385,257},{258,386},{386,258},{259,3... | collective-permute-start | bytes 73736 | tf_op jit(solution)/shard_map/ppermute | solution.py:255
  77.9 7.1 %collective-permute-start.3 = (f32[48,128]{1,0:T(8,128)S(1)}, f32[48,128]{1,0:T(8,128)S(1)}, u32[]{:S(2)}, u32[]{:S(2)}) collective-permute-start(f32[48,128]{1,0:T(8,128)S(1)} %get-tuple-element.11.total), channel_id=1, source_target_pairs={{256,128},{257,129},{258,130},{259,131},{260,132},{261,133},{262,1... | collective-permute-start | bytes 73736 | tf_op jit(solution)/shard_map/ppermute | solution.py:252
  80.0 6.8 %collective-permute-start.4 = (f32[48,128]{1,0:T(8,128)S(1)}, f32[48,128]{1,0:T(8,128)S(1)}, u32[]{:S(2)}, u32[]{:S(2)}) collective-permute-start(f32[48,128]{1,0:T(8,128)S(1)} %shard_map.46), channel_id=1, source_target_pairs={{128,256},{0,384},{129,257},{1,385},{130,258},{2,386},{131,259},{3... | collective-permute-start | bytes 73736 | tf_op jit(solution)/shard_map/ppermute | solution.py:254

commit v12 on v11

--- a/solution.py
+++ b/solution.py
@@ -116,21 +116,29 @@
     return jnp.concatenate([top, bottom], axis=0)
 
 
-def tile_zero_kernel(prior, raw, out, total):
-    step = pl.program_id(0)
-    part = lax.dot_general(prior[...], raw[...], NT, preferred_element_type=F32)
-
-    @pl.when(step == 0)
-    def _():
-        total[...] = part
-
-    @pl.when(step > 0)
-    def _():
-        total[...] += part
-
-    @pl.when(step == STEPS - 1)
-    def _():
-        pack_rows(total[...], out)
+def tile_zero_kernel(prior, raw, out, prior_near, raw_near, total, sems):
+    width = 2048 // STEPS
+    copies = []
+    for step in range(STEPS):
+        group = []
+        for i in range(4):
+            source, target = (prior, prior_near) if i < 2 else (raw, raw_near)
+            piece = (pl.ds(i % 2 * 256, 256), pl.ds(step * width, width))
+            group.append(pltpu.make_async_copy(source.at[piece], target.at[piece], sems.at[step * 4 + i]))
+        copies.append(group)
+    for group in copies:
+        for copy in group:
+            copy.start()
+    for step, group in enumerate(copies):
+        for copy in group:
+            copy.wait()
+        columns = slice(step * width, (step + 1) * width)
+        part = lax.dot_general(prior_near[:, columns], raw_near[:, columns], NT, preferred_element_type=F32)
+        if step == 0:
+            total[...] = part
+        else:
+            total[...] += part
+    pack_rows(total[...], out)
 
 
 def tile_one_kernel(prior, raw_next, prior_last, raw, out):
@@ -229,14 +237,13 @@
     raw_next = lax.ppermute(raw, LAG + PAR, down)
     prior_last = lax.ppermute(prior, LAG + PAR, up)
 
-    piece = pl.BlockSpec((512, 2048 // STEPS), lambda step: (0, step))
-    zero = pl.pallas_call(
+    full = pltpu.VMEM((512, 2048), jnp.bfloat16)
+    zero, prior, raw = pl.pallas_call(
         tile_zero_kernel,
-        out_shape=shape(4, 2, 8, 4224),
-        grid=(STEPS,),
-        in_specs=[piece, piece],
-        out_specs=VMEM,
-        scratch_shapes=[pltpu.VMEM((512, 512), F32)],
+        out_shape=(shape(4, 2, 8, 4224), full, full),
+        in_specs=[pl.BlockSpec(memory_space=pltpu.HBM)] * 2,
+        out_specs=(VMEM,) * 3,
+        scratch_shapes=[pltpu.VMEM((512, 512), F32), pltpu.SemaphoreType.DMA((STEPS * 4,))],
         compiler_params=pltpu.CompilerParams(vmem_limit_bytes=8 * 2**20),
     )(far(prior), far(raw))
     zero = exchange_short(zero.reshape(8, 8, 4224), PAR).reshape(4, 2, 8, 4224)

time: 101 us -> 104 us (1.030)
  starting transfers between devices: 17.5 us -> 21.5 us
  Pallas kernels: 7.29 us -> 5.93 us
    ppermute x1, starting transfers between devices: 5.02 us -> 8.97 us  [body(): crossed = lax.ppermute(both, 'zh', [(1, 2), (0, 3)])]
    pallas_call x1, Pallas kernels: 4.41 us -> 3.06 us  [body(): pl.pallas_call(tile_zero_kernel, out_shape=(shape(4, 2, 8, 4224), full, f...]
  transfers between devices with their start and end apart: 6 -> 6, of which waited for: 2 -> 2; matrix products, arithmetic and copies ran while one was open for 0% -> 0% of each run, Pallas kernels for 4% -> 3%
where the time goes in v12:
time: 104 us
  blocking collectives  72.2 us (69%)
  starting transfers between devices  21.5 us (21%)
  Pallas kernels  5.93 us (6%)
  waiting for transfers between devices  3.16 us (3%)
    all_to_all x5, blocking collectives, exchange(): return lax.all_to_all(value, axes, 0, 0, tiled=True)  72.2 us
    ppermute x1, starting transfers between devices, body(): early = lax.ppermute(total, 'zh', [(0, 1), (1, 0)])  9.1 us
    ppermute x1, starting transfers between devices, body(): crossed = lax.ppermute(both, 'zh', [(1, 2), (0, 3)])  8.97 us
    pallas_call x1, Pallas kernels, body(): pl.pallas_call(tile_zero_kernel, out_shape=(shape(4, 2, 8, 4224), full, f...  3.06 us
    pallas_call x7, Pallas kernels, call(): pl.pallas_call(kernel, out_shape=out_shape, in_specs=[VMEM] * len(args),...  2.87 us
  transfers between devices with their start and end apart: 6, of which 2 were waited for; matrix products, arithmetic and copies ran while one was open for 0% of the time, Pallas kernels for 3%

profile of v12, /device:TPU:2, one launch (start us, length us, event | category | flops | bytes accessed | tf_op | source)
XLA Modules:
  0.0 103.9 jit_solution(6116343998326341784)
XLA Ops:
  0.6 1.3 %collective-permute-start = (bf16[512,2048]{1,0:T(8,128)(2,1)}, bf16[512,2048]{1,0:T(8,128)(2,1)S(1)}, u32[]{:S(2)}, u32[]{:S(2)}) collective-permute-start(bf16[512,2048]{1,0:T(8,128)(2,1)} %bitcast.14), channel_id=1, source_target_pairs={{8,0},{10,2},{12,4},{14,6},{16,8},{18,10},{20,12},{22,14},{24,16},... | collective-permute-start | bytes 6291464 | tf_op jit(solution)/shard_map/ppermute | solution.py:237
  1.9 0.8 collective-permute-start.1
  2.7 3.1 %shard_map.41 = (f32[4,2,8,4224]{3,2,1,0:T(8,128)S(1)}, bf16[512,2048]{1,0:T(8,128)(2,1)S(1)}, bf16[512,2048]{1,0:T(8,128)(2,1)S(1)}) custom-call(bf16[512,2048]{1,0:T(8,128)(2,1)} %bitcast.17, bf16[512,2048]{1,0:T(8,128)(2,1)} %bitcast.15), custom_call_target="tpu_custom_call" | custom-call | tf_op jit(solution)/shard_map/pallas_call | solution.py:241
  5.8 0.1 convert_element_type.20
  5.9 17.4 %all_to_all.25 = f16[8,8,4224]{2,1,0:T(8,128)(2,1)S(1)} all-to-all(f16[8,8,4224]{2,1,0:T(8,128)(2,1)S(1)} %bitcast.12), channel_id=1, replica_groups=mesh['zh'=4,'zl'=4,'y'=4,'x'=4,'core'=2] {'x','core'}, dimensions={0} | all-to-all | bytes 1081344 | tf_op jit(solution)/shard_map/all_to_all | solution.py:225
  23.2 0.1 convert.2.parts
  23.3 0.1 shard_map.42
  23.4 9.7 %all_to_all.26.zero = f32[4,16,512]{2,1,0:T(8,128)S(1)} all-to-all(f32[4,16,512]{2,1,0:T(8,128)S(1)} %bitcast.9), channel_id=1, replica_groups=mesh['zh'=4,'zl'=4,'y'=4,'x'=4,'core'=2] {'y'}, dimensions={0} | all-to-all | bytes 262144 | tf_op jit(solution)/shard_map/all_to_all | solution.py:225
  33.1 0.0 collective-permute-done.raw_next
  33.1 0.0 collective-permute-done.1.prior_last
  33.1 1.5 %shard_map.43 = f32[4,4,2,8,1152]{4,3,2,1,0:T(8,128)S(1)} custom-call(bf16[512,2048]{1,0:T(8,128)(2,1)S(1)} %get-tuple-element.12.prior, bf16[512,2048]{1,0:T(8,128)(2,1)S(1)} %collective-permute-done.raw_next, bf16[512,2048]{1,0:T(8,128)(2,1)S(1)} %collective-permute-done.1.prior_last, bf16[512,2048]{1,0:T(8,128)(2,1)S(1)} %get-tuple-element.15.raw), custom_call_target="tpu_custom_call" | custom-call | tf_op jit(solution)/shard_map/pallas_call | solution.py:28
  34.6 0.1 convert_element_type.22
  34.6 18.0 %all_to_all.27 = f16[32,8,1152]{2,1,0:T(8,128)(2,1)S(1)} all-to-all(f16[32,8,1152]{2,1,0:T(8,128)(2,1)S(1)} %bitcast.10), channel_id=1, replica_groups=mesh['zh'=4,'zl'=4,'y'=4,'x'=4,'core'=2] {'y','x','core'}, dimensions={0} | all-to-all | bytes 1179648 | tf_op jit(solution)/shard_map/all_to_all | solution.py:225
  52.6 0.1 convert.3.one
  52.7 0.4 shard_map.44
  53.1 14.0 %all_to_all.28 = f16[4,168,128]{2,1,0:T(8,128)(2,1)S(1)} all-to-all(f16[4,168,128]{2,1,0:T(8,128)(2,1)S(1)} %convert_element_type.24), channel_id=1, replica_groups=mesh['zh'=4,'zl'=4,'y'=4,'x'=4,'core'=2] {'zl'}, dimensions={0} | all-to-all | bytes 344064 | tf_op jit(solution)/shard_map/all_to_all | solution.py:225
  67.1 0.2 shard_map.45
  67.3 9.1 %collective-permute-start.2 = (f32[48,128]{1,0:T(8,128)S(1)}, f32[48,128]{1,0:T(8,128)S(1)}, u32[]{:S(2)}, u32[]{:S(2)}) collective-permute-start(f32[48,128]{1,0:T(8,128)S(1)} %get-tuple-element.17.total), channel_id=1, source_target_pairs={{0,128},{128,0},{1,129},{129,1},{2,130},{130,2},{3,131},{131,3},{4... | collective-permute-start | bytes 73736 | tf_op jit(solution)/shard_map/ppermute | solution.py:258
  76.5 0.7 collective-permute-start.3
  77.1 0.7 collective-permute-start.5
  77.8 1.4 %collective-permute-done.2.other.early = f32[48,128]{1,0:T(8,128)S(1)} collective-permute-done((f32[48,128]{1,0:T(8,128)S(1)}, f32[48,128]{1,0:T(8,128)S(1)}, u32[]{:S(2)}, u32[]{:S(2)}) %collective-permute-start.2) | collective-permute-done | bytes 24608 | tf_op jit(solution)/shard_map/ppermute | solution.py:258
  79.2 9.0 %collective-permute-start.4 = (f32[48,128]{1,0:T(8,128)S(1)}, f32[48,128]{1,0:T(8,128)S(1)}, u32[]{:S(2)}, u32[]{:S(2)}) collective-permute-start(f32[48,128]{1,0:T(8,128)S(1)} %shard_map.46), channel_id=1, source_target_pairs={{128,256},{0,384},{129,257},{1,385},{130,258},{2,386},{131,259},{3... | collective-permute-start | bytes 73736 | tf_op jit(solution)/shard_map/ppermute | solution.py:261
  88.2 0.0 collective-permute-done.3.back
  88.2 0.0 collective-permute-done.5.own
  88.2 1.8 %collective-permute-done.4.crossed = f32[48,128]{1,0:T(8,128)S(1)} collective-permute-done((f32[48,128]{1,0:T(8,128)S(1)}, f32[48,128]{1,0:T(8,128)S(1)}, u32[]{:S(2)}, u32[]{:S(2)}) %collective-permute-start.4) | collective-permute-done | bytes 24608 | tf_op jit(solution)/shard_map/ppermute | solution.py:261
  90.0 13.2 %all_to_all.29.rows = f32[16,32,128]{2,1,0:T(8,128)S(1)} all-to-all(f32[16,32,128]{2,1,0:T(8,128)S(1)} %shard_map.47), channel_id=1, replica_groups=mesh['zh'=4,'zl'=4,'y'=4,'x'=4,'core'=2] {'zl','y'}, dimensions={0} | all-to-all | bytes 524288 | tf_op jit(solution)/shard_map/all_to_all | solution.py:225
  103.2 0.7 shard_map.48
  (4 shorter events, 0.1 us)
Async XLA Ops:
  0.6 32.5 %collective-permute-start = (bf16[512,2048]{1,0:T(8,128)(2,1)}, bf16[512,2048]{1,0:T(8,128)(2,1)S(1)}, u32[]{:S(2)}, u32[]{:S(2)}) collective-permute-start(bf16[512,2048]{1,0:T(8,128)(2,1)} %bitcast.14), channel_id=1, source_target_pairs={{8,0},{10,2},{12,4},{14,6},{16,8},{18,10},{20,12},{22,14},{24,16},... | collective-permute-start | bytes 6291464 | tf_op jit(solution)/shard_map/ppermute | solution.py:237
  1.9 31.2 %collective-permute-start.1 = (bf16[512,2048]{1,0:T(8,128)(2,1)}, bf16[512,2048]{1,0:T(8,128)(2,1)S(1)}, u32[]{:S(2)}, u32[]{:S(2)}) collective-permute-start(bf16[512,2048]{1,0:T(8,128)(2,1)} %bitcast.16), channel_id=1, source_target_pairs={{1,9},{3,11},{5,13},{7,15},{9,17},{11,19},{13,21},{15,23},{17,25},... | collective-permute-start | bytes 6291464 | tf_op jit(solution)/shard_map/ppermute | solution.py:238
  67.3 11.8 %collective-permute-start.2 = (f32[48,128]{1,0:T(8,128)S(1)}, f32[48,128]{1,0:T(8,128)S(1)}, u32[]{:S(2)}, u32[]{:S(2)}) collective-permute-start(f32[48,128]{1,0:T(8,128)S(1)} %get-tuple-element.17.total), channel_id=1, source_target_pairs={{0,128},{128,0},{1,129},{129,1},{2,130},{130,2},{3,131},{131,3},{4... | collective-permute-start | bytes 73736 | tf_op jit(solution)/shard_map/ppermute | solution.py:258
  76.5 11.7 %collective-permute-start.3 = (f32[48,128]{1,0:T(8,128)S(1)}, f32[48,128]{1,0:T(8,128)S(1)}, u32[]{:S(2)}, u32[]{:S(2)}) collective-permute-start(f32[48,128]{1,0:T(8,128)S(1)} %get-tuple-element.17.total), channel_id=1, source_target_pairs={{256,128},{257,129},{258,130},{259,131},{260,132},{261,133},{262,1... | collective-permute-start | bytes 73736 | tf_op jit(solution)/shard_map/ppermute | solution.py:259
  77.1 11.1 %collective-permute-start.5 = (f32[48,128]{1,0:T(8,128)S(1)}, f32[48,128]{1,0:T(8,128)S(1)}, u32[]{:S(2)}, u32[]{:S(2)}) collective-permute-start(f32[48,128]{1,0:T(8,128)S(1)} %get-tuple-element.17.total), channel_id=1, source_target_pairs={{256,384},{384,256},{257,385},{385,257},{258,386},{386,258},{259,3... | collective-permute-start | bytes 73736 | tf_op jit(solution)/shard_map/ppermute | solution.py:262
  79.2 10.7 %collective-permute-start.4 = (f32[48,128]{1,0:T(8,128)S(1)}, f32[48,128]{1,0:T(8,128)S(1)}, u32[]{:S(2)}, u32[]{:S(2)}) collective-permute-start(f32[48,128]{1,0:T(8,128)S(1)} %shard_map.46), channel_id=1, source_target_pairs={{128,256},{0,384},{129,257},{1,385},{130,258},{2,386},{131,259},{3... | collective-permute-start | bytes 73736 | tf_op jit(solution)/shard_map/ppermute | solution.py:261
